TPU v7x, 256 devices: a whole 4x4x8 slice. The times are simulated.
256 devices in a mesh: heads: 16 (over x_lo, y, core), keys: 16 (over z, x_hi).
Axes of the slice: x: 4 (x_hi: 2, x_lo: 2; x = x_hi * 2 + x_lo), y: 4, z: 8, core: 2. Of those that a mesh axis runs over, the one named last changes fastest.
Arguments:
- main_query: bfloat16 [256, 128, 576], P(None, 'heads'), may hold values from -5 to 5
- latent_keys: bfloat16 [32768, 576], P('keys'), may hold values from -16 to 16
- index_query: bfloat16 [256, 64, 128], P('heads'), may hold values from -1 to 1
- index_keys: bfloat16 [32768, 128], P('keys'), may hold values from -20 to 20
- index_weight: float32 [256, 64], P('heads'), may hold values from -0.15 to 1
- query_pos: int32 [256], replicated, may hold values from 4096 to 32767, as said below
- kl_weight: float32 [256], P('heads'), may hold values from 2 to 16
Outputs:
- index_query_grad: float32 [256, 64, 128], P('heads')
- index_key_grad: float32 [32768, 128], P('keys')
- index_weight_grad: float32 [256, 64], P('heads')
Inputs may be any that keep to these rules, and one draw needn't show every extreme that they name: Query q sees the keys at positions 0 to query_pos[q]; some query sees all 32768 keys and some sees exactly the first 4097.
All inputs are finite; a program needn't handle non-finite values.
Results may differ from a plain program's by a relative error of at most 0.005.
Values sent between devices are 32-bit elements; how exact they have to be, the bound alone decides.
A program may use at most 128 MiB of HBM per device.

v0:
```python
import jax
import jax.numpy as jnp
from jax import lax
from jax.sharding import PartitionSpec as P

H = 128


softmax_scale = 192.0 ** (-0.5)
masked_fill = -1e30


def contract_last(left_side, right_side):
    return lax.dot_general(
        left_side, right_side, (((1,), (1,)), ((), ())), preferred_element_type=jnp.float32
    )


def shards(main_query, latent_keys, index_query, index_keys, index_weight, query_pos, kl_weight):
    query_count, head_local, feature_width = main_query.shape
    key_local = latent_keys.shape[0]
    row_local, index_heads, index_width = index_query.shape
    key_first = lax.axis_index("keys") * key_local
    key_index = key_first + lax.iota(jnp.int32, key_local)
    visible = key_index[None, :] <= query_pos[:, None]
    row_first = lax.axis_index("heads") * row_local
    row_pos = lax.dynamic_slice_in_dim(query_pos, row_first, row_local)
    row_visible = key_index[None, :] <= row_pos[:, None]
    main_scores = contract_last(
        main_query.reshape(query_count * head_local, feature_width), latent_keys
    )
    main_scores = main_scores.reshape(query_count, head_local, key_local) * softmax_scale
    main_scores = jnp.where(visible[:, None, :], main_scores, masked_fill)
    index_logits = contract_last(
        index_query.reshape(row_local * index_heads, index_width), index_keys
    )
    index_logits = index_logits.reshape(row_local, index_heads, key_local)
    active = jnp.maximum(index_logits, 0.0)
    index_scores = jnp.einsum("qj,qjk->qk", index_weight, active, precision=lax.Precision.HIGHEST)
    index_scores = jnp.where(row_visible, index_scores, masked_fill)
    main_local = jnp.max(main_scores, axis=2)
    index_local = jnp.max(index_scores, axis=1)
    main_maxima, index_maxima = lax.pmax((main_local, index_local), "keys")
    main_sum = jnp.sum(
        jnp.where(visible[:, None, :], jnp.exp(main_scores - main_maxima[:, :, None]), 0.0), axis=2
    )
    index_sum = jnp.sum(
        jnp.where(row_visible, jnp.exp(index_scores - index_maxima[:, None]), 0.0), axis=1
    )
    main_totals, index_totals = lax.psum((main_sum, index_sum), "keys")
    main_probs = (
        jnp.where(visible[:, None, :], jnp.exp(main_scores - main_maxima[:, :, None]), 0.0)
        / main_totals[:, :, None]
    )
    partial_value = jnp.sum(main_probs, axis=1)
    summed = lax.psum(partial_value, "heads")
    target = lax.dynamic_slice_in_dim(summed, row_first, row_local, 0)
    target = target / H
    index_probs = (
        jnp.where(row_visible, jnp.exp(index_scores - index_maxima[:, None]), 0.0)
        / index_totals[:, None]
    )
    index_delta = kl_weight[:, None] * (index_probs - target)
    weight_grad = jnp.einsum("qk,qjk->qj", index_delta, active, precision=lax.Precision.HIGHEST)
    slopes = jnp.where(
        index_logits > 0.0, index_delta[:, None, :] * index_weight[:, :, None], 0.0
    ).astype(jnp.bfloat16)
    flattened = slopes.reshape(row_local * index_heads, key_local)
    query_grad = jnp.dot(flattened, index_keys, preferred_element_type=jnp.float32).reshape(
        row_local, index_heads, index_width
    )
    key_grad = lax.dot_general(
        flattened,
        index_query.reshape(row_local * index_heads, index_width),
        (((0,), (0,)), ((), ())),
        preferred_element_type=jnp.float32,
    )
    query_grad, weight_grad = lax.psum((query_grad, weight_grad), "keys")
    key_grad = lax.psum(key_grad, "heads")
    return (query_grad, key_grad, weight_grad)


def solution(mesh):
    placed = (
        P(None, "heads", None),
        P("keys", None),
        P("heads", None, None),
        P("keys", None),
        P("heads", None),
        P(),
        P("heads"),
    )
    return jax.shard_map(
        shards,
        mesh=mesh,
        in_specs=placed,
        out_specs=(P("heads", None, None), P("keys", None), P("heads", None)),
        check_vma=False,
    )
```

profile of v0, /device:TPU:1, one launch (start us, length us, event | category | flops | bytes accessed | tf_op | source)
XLA Modules:
  0.0 565.1 jit_solution(11761084762094805328)
XLA Ops:
  7.3 0.9 dynamic_slice.6
  8.2 1.0 broadcast_compare_fusion
  9.2 3.3 fusion.8
  12.6 3.2 copy-done.1
  15.8 4.6 fusion.4
  20.4 0.2 fusion.28
  20.6 11.6 %fusion = (f32[256,8]{0,1:T(8,128)S(1)}, f32[256,8,2048]{2,0,1:T(8,128)}) fusion(pred[256,2048]{1,0:T(8,128)(4,1)S(1)} %broadcast_compare_fusion, bf16[256,8,576]{0,2,1:T(8,128)(2,1)S(1)} %copy-done, bf16[2048,576]{0,1:T(8,128)(2,1)S(1)} %copy-done.8), kind=kOutput, calls=%fused_computation.3 | convolution fusion | flops 4844419072 | bytes 22028288 | tf_op jit(solution)/shard_map/dot_general | solution.py:14
  32.2 39.7 %all-reduce.1 = (f32[256,8]{0,1:T(8,128)S(1)}, f32[16]{0:T(128)S(1)}) all-reduce(f32[256,8]{0,1:T(8,128)S(1)} %get-tuple-element.7, f32[16]{0:T(128)S(1)} %fusion.28), channel_id=1, replica_groups=mesh['heads'=16,'keys'=16] {'keys'}, use_global_device_ids=true, to_apply=%region_5.6 | all-reduce | flops 2064 | bytes 16512 | tf_op jit(solution)/shard_map/pmax | solution.py:43
  71.9 0.2 fusion.29
  72.1 8.4 %fusion.1 = f32[256,8]{0,1:T(8,128)S(1)} fusion(f32[256,8,2048]{2,0,1:T(8,128)} %get-tuple-element.8, f32[256,8]{0,1:T(8,128)S(1)} %get-tuple-element.5, pred[256,2048]{1,0:T(8,128)(4,1)S(1)} %broadcast_compare_fusion), kind=kLoop, calls=%fused_computation.4 | loop fusion | flops 20969472 | bytes 17317888 | tf_op jit(solution)/shard_map/reduce_sum | solution.py:44
  80.5 31.6 %all-reduce = (f32[256,8]{0,1:T(8,128)}, f32[16]{0:T(128)}) all-reduce(f32[256,8]{0,1:T(8,128)S(1)} %fusion.1, f32[16]{0:T(128)S(1)} %fusion.29), channel_id=1, replica_groups=mesh['heads'=16,'keys'=16] {'keys'}, use_global_device_ids=true, to_apply=%region_7.8 | all-reduce | flops 2064 | bytes 16512 | tf_op jit(solution)/shard_map/psum | solution.py:50
  112.2 10.2 %divide_reduce_fusion = f32[256,2048]{1,0:T(8,128)} fusion(f32[256,8,2048]{2,0,1:T(8,128)} %get-tuple-element.8, f32[256,8]{0,1:T(8,128)} %get-tuple-element.3, f32[256,8]{0,1:T(8,128)S(1)} %get-tuple-element.5, pred[256,2048]{1,0:T(8,128)(4,1)S(1)} %broadcast_compare_fusion), kind=kLoop, calls=%fused_computation.2 | loop fusion | flops 24641536 | bytes 19415040 | tf_op jit(solution)/shard_map/reduce_sum | solution.py:55
  122.4 0.0 all-reduce.8.cloned.1.call-start
  122.4 140.4 %all-reduce.6.cloned.1.call-done = f32[256,2048]{1,0:T(8,128)} async-done(((f32[256,2048]{1,0:T(8,128)}), f32[256,2048]{1,0:T(8,128)}) %all-reduce.6.cloned.1.call-update) | async-done | bytes 2097168 | tf_op jit(solution)/shard_map/psum | solution.py:56
  262.9 1.1 subtract_multiply_fusion
  264.0 3.1 fusion.7
  267.1 0.0 all-reduce.10.cloned.1.call-start
  267.2 3.6 fusion.19
  270.8 9.0 %fusion.2 = f32[16,1,64]{2,1,0:T(1,128)S(1)} fusion(f32[16,64,2048]{2,1,0:T(8,128)} %copy-done.1, f32[16,2048,1]{1,0,2:T(8,128)S(1)} %bitcast.34), kind=kOutput, calls=%fused_computation.8 | convolution fusion | flops 27262976 | bytes 8523776 | tf_op jit(solution)/shard_map/qk,qjk->qj/dot_general | solution.py:64
  279.8 36.5 %psum.47 = f32[16,64]{1,0:T(8,128)} all-reduce(f32[16,64]{1,0:T(8,128)S(1)} %bitcast.35), channel_id=1, replica_groups=mesh['heads'=16,'keys'=16] {'keys'}, use_global_device_ids=true, to_apply=%region_12.13 | all-reduce | flops 1024 | bytes 8192 | tf_op jit(solution)/shard_map/psum | solution.py:78
  316.4 100.5 %all-reduce.8.cloned.1.call-done = f32[16,64,128]{2,1,0:T(8,128)} async-done(((f32[16,64,128]{2,1,0:T(8,128)}), f32[16,64,128]{2,1,0:T(8,128)}) %all-reduce.8.cloned.1.call-update) | async-done | bytes 524304 | tf_op jit(solution)/shard_map/psum | solution.py:78
  416.9 137.6 %all-reduce.10.cloned.1.call-done = f32[2048,128]{1,0:T(8,128)} async-done(((f32[2048,128]{1,0:T(8,128)}), f32[2048,128]{1,0:T(8,128)}) %all-reduce.10.cloned.1.call-update) | async-done | bytes 1048592 | tf_op jit(solution)/shard_map/psum | solution.py:79
  554.5 1.9 copy.28
  556.3 2.3 copy.29
  (22 shorter events, 0.1 us)
Async XLA Ops:
  7.2 13.4 %copy-start = (bf16[256,8,576]{0,2,1:T(8,128)(2,1)S(1)}, bf16[256,8,576]{0,2,1:T(8,128)(2,1)}, u32[]{:S(2)}) copy-start(bf16[256,8,576]{0,2,1:T(8,128)(2,1)} %param.7) | copy-start | bytes 7077892
  7.2 8.6 %copy-start.4 = (f32[16,64]{1,0:T(8,128)S(1)}, f32[16,64]{1,0:T(8,128)}, u32[]{:S(2)}) copy-start(f32[16,64]{1,0:T(8,128)} %param.11) | copy-start | bytes 12292
  7.2 255.7 %all-reduce.6.cloned.1.call-start = ((), (), s32[]{:S(2)}) async-start(), calls=%async_computation | async-start | bytes 4194304 | tf_op jit(solution)/shard_map/psum | solution.py:56
  8.2 63.8 %copy-start.6 = (s32[16]{0:T(128)}, s32[16]{0:T(128)S(1)}, u32[]{:S(2)}) copy-start(s32[16]{0:T(128)S(1)} %dynamic_slice.6) | copy-start | bytes 196
  9.2 11.4 %copy-start.8 = (bf16[2048,576]{0,1:T(8,128)(2,1)S(1)}, bf16[2048,576]{0,1:T(8,128)(2,1)}, u32[]{:S(2)}) copy-start(bf16[2048,576]{0,1:T(8,128)(2,1)} %param.8) | copy-start | bytes 7077892
  12.5 3.2 copy-start.1
  71.9 8.6 %copy-start.7 = (f32[16]{0:T(128)}, f32[16]{0:T(128)S(1)}, u32[]{:S(2)}) copy-start(f32[16]{0:T(128)S(1)} %get-tuple-element.6) | copy-start | bytes 196
  112.2 151.8 %copy-start.2 = (bf16[2048,128]{1,0:T(8,128)(2,1)S(1)}, bf16[2048,128]{1,0:T(8,128)(2,1)}, u32[]{:S(2)}) copy-start(bf16[2048,128]{1,0:T(8,128)(2,1)} %param.10) | copy-start | bytes 1572868
  122.4 294.5 %all-reduce.8.cloned.1.call-start = ((), (), s32[]{:S(2)}) async-start(), calls=%async_computation.1 | async-start | bytes 1048576 | tf_op jit(solution)/shard_map/psum | solution.py:78
  264.0 3.2 copy-start.3
  264.0 3.2 copy-start.5
  267.1 287.3 %all-reduce.10.cloned.1.call-start = ((), (), s32[]{:S(2)}) async-start(), calls=%async_computation.2 | async-start | bytes 2097152 | tf_op jit(solution)/shard_map/psum | solution.py:79
Sparse Core Ops, SparseCore 0:
  122.5 140.3 all-reduce.5
  267.3 149.5 all-reduce.7
  420.1 134.3 all-reduce.9
where the time goes:
time: 566 us; the launch traced here: 565 us
  waiting for transfers between devices  379 us (67%)
  blocking collectives  108 us (19%)
  matrix products  35.3 us (6%)
  other arithmetic  21.1 us (4%)
  between operations  13.9 us (2%)
  local copies, waits for them, and re-layouts  8.32 us (1%)
    psum x1, waiting for transfers between devices, shards(): summed = lax.psum(partial_value, 'heads')  140 us
    psum x1, waiting for transfers between devices, shards(): key_grad = lax.psum(key_grad, 'heads')  138 us
    psum x1, waiting for transfers between devices, shards(): query_grad, weight_grad = lax.psum((query_grad, weight_grad), 'keys')  101 us
    pmax x1, blocking collectives, shards(): main_maxima, index_maxima = lax.pmax((main_local, index_local), 'keys')  39.7 us
    psum x1, blocking collectives, shards(): query_grad, weight_grad = lax.psum((query_grad, weight_grad), 'keys')  36.5 us
    psum x1, blocking collectives, shards(): main_totals, index_totals = lax.psum((main_sum, index_sum), 'keys')  31.6 us
    dot_general x2, matrix products, contract_last(): lax.dot_general(left_side, right_side, (((1,), (1,)), ((), ())), preferre...  15 us
  transfers between devices with their start and end apart: 3, of which 3 were waited for; matrix products, arithmetic and copies ran while one was open for 2% of the time, Pallas kernels for 0%

commit v1 on v0

v1 whole, which is shorter than its diff:
```python
import jax
import jax.numpy as jnp
from jax import lax
from jax.experimental import pallas as pl
from jax.experimental.pallas import tpu as pltpu
from jax.sharding import PartitionSpec as P

H = 128
SCALE = 192.0 ** (-0.5)
MASKED = -1e30
FLOOR = -1e29
MESH = pl.DeviceIdType.MESH
LAG = 3
NT = (((1,), (1,)), ((), ()))
F32 = jnp.float32
BF16 = jnp.bfloat16


def lanes(t):
    return slice(t * 128, (t + 1) * 128)


def fused(
    pos_s, kl_s, mq, lk, iq, ik, iw,
    qg_out, kg_out, wg_out,
    s_ref, e_ref, st_ref, stat_mine, stat_all,
    tp_ref, tc_ref, tx_ref, ty_ref,
    lg_ref, wpad_ref, wcol_ref, iqt_ref, is_ref, ie_ref, ist_mine, ist_all, d_ref,
    sl_ref, wgc_ref, qg_part, qg_recv, qg_xh, qg_all,
    kp_ref, kc_ref, kx_ref, ky_ref, kg_all,
    stat_ss, stat_rs, ist_ss, ist_rs,
    tc_ss, tc_rs, tx_ss, tx_rs, ty_ss, ty_rs,
    qg_ss, qg_rs, xh_ss, xh_rs, qa_ss, qa_rs,
    kc_ss, kc_rs, kx_ss, kx_rs, ky_ss, ky_rs, ka_ss, ka_rs,
):
    h = lax.axis_index("heads")
    k = lax.axis_index("keys")
    core, y, x = h % 2, (h // 2) % 4, h // 8
    z, xh = k // 2, k % 2
    key_first = k * 2048
    partner = x * 8 + y * 2 + (1 - core)
    across = (1 - x) * 8 + y * 2 + core

    def along_y(off):
        return x * 8 + ((y + off) % 4) * 2 + core

    def chip(b):
        return ((x + 1 - b // 4) % 2) * 4 + (y + 3 - b % 4) % 4

    barrier = pltpu.get_barrier_semaphore()
    for r in range(1, 16):
        pl.semaphore_signal(barrier, inc=1, device_id={"keys": (k + r) % 16}, device_id_type=MESH)
    for peer in (partner, across, along_y(1), along_y(2), along_y(3)):
        pl.semaphore_signal(barrier, inc=1, device_id={"heads": peer}, device_id_type=MESH)

    lane = lax.broadcasted_iota(jnp.int32, (1, 128), 1)

    wpad_ref[...] = jnp.zeros((128, 128), F32)
    wpad_ref[0:16, 0:64] = iw[...]
    wturned = jnp.transpose(wpad_ref[...])
    for q in range(16):
        wcol_ref[q * 64:(q + 1) * 64, :] = jnp.broadcast_to(wturned[0:64, q:q + 1], (64, 128))
    for i in range(8):
        iqt_ref[:, lanes(i)] = jnp.transpose(iq[lanes(i), :].astype(F32)).astype(BF16)

    def to_heads(src, dst, ss, rs, peer):
        return pltpu.make_async_remote_copy(
            src_ref=src, dst_ref=dst, send_sem=ss, recv_sem=rs,
            device_id={"heads": peer}, device_id_type=MESH,
        )

    def to_keys(src, dst, ss, rs, peer):
        return pltpu.make_async_remote_copy(
            src_ref=src, dst_ref=dst, send_sem=ss, recv_sem=rs,
            device_id={"keys": peer}, device_id_type=MESH,
        )

    def take(ref, sem):
        pltpu.make_async_copy(ref, ref, sem).wait()

    def score_block(b):
        c = chip(b)
        r0 = pl.multiple_of(c * 256, 256)
        s_ref[...] = lax.dot_general(mq[pl.ds(r0, 256), :], lk[...], NT, preferred_element_type=F32)

        def piece(i, carry):
            rows = pl.ds(pl.multiple_of(i * 64, 64), 64)
            posv = jnp.concatenate(
                [jnp.full((8, 128), pos_s[c * 32 + i * 8 + j] - key_first, jnp.int32) for j in range(8)],
                axis=0,
            )
            top = jnp.full((64, 128), FLOOR, F32)
            for t in range(16):
                v = jnp.where(lane + t * 128 <= posv, s_ref[rows, lanes(t)], MASKED)
                s_ref[rows, lanes(t)] = v
                top = jnp.maximum(top, v)
            mcol = jnp.broadcast_to(jnp.max(top, axis=1, keepdims=True), (64, 128))
            total = jnp.zeros((64, 128), F32)
            erows = pl.ds(pl.multiple_of(r0 + i * 64, 64), 64)
            for t in range(16):
                e = jnp.exp((s_ref[rows, lanes(t)] - mcol) * SCALE)
                total = total + e
                e_ref[erows, lanes(t)] = e.astype(BF16)
            lcol = jnp.broadcast_to(jnp.sum(total, axis=1, keepdims=True), (64, 128))
            st_ref[rows, :] = jnp.where(lane == 0, mcol, lcol)
            return carry

        lax.fori_loop(0, 4, piece, 0)
        stat_mine[b] = jnp.transpose(st_ref[...])[0:2, :]

    def send_stats(b):
        for r in range(1, 16):
            to_keys(stat_mine.at[b], stat_all.at[b, r - 1], stat_ss.at[b], stat_rs.at[b], (k + r) % 16).start()

    def target_block(b):
        take(stat_all.at[b], stat_rs.at[b])
        mine = stat_mine[b]
        m0, l0 = mine[0:1, :], mine[1:2, :]
        ms = [stat_all[b, r][0:1, :] for r in range(15)]
        ls = [stat_all[b, r][1:2, :] for r in range(15)]
        top = m0
        for m in ms:
            top = jnp.maximum(top, m)
        share = jnp.exp((m0 - top) * SCALE)
        total = l0 * share
        for m, l in zip(ms, ls):
            total = total + l * jnp.exp((m - top) * SCALE)
        w = share / (total * float(H))
        high = w.astype(BF16).astype(F32)
        low = w - high
        mine_of = lax.broadcasted_iota(jnp.int32, (32, 256), 1) // 8 == lax.broadcasted_iota(
            jnp.int32, (32, 256), 0
        )
        a = jnp.concatenate([jnp.where(mine_of, high, 0.0), jnp.where(mine_of, low, 0.0)], axis=0)
        r0 = pl.multiple_of(chip(b) * 256, 256)
        got = jnp.dot(a.astype(BF16), e_ref[pl.ds(r0, 256), :], preferred_element_type=F32)
        got = got[0:32, :] + got[32:64, :]
        tp_ref[b, 0] = got[0:16, :]
        tp_ref[b, 1] = got[16:32, :]
        to_heads(tp_ref.at[b, 1 - core], tc_ref.at[b], tc_ss.at[b], tc_rs.at[b], partner).start()

    def cross_x(b, p_ref, c_ref, x_ref, c_rs, x_ss, x_rs):
        take(c_ref.at[b], c_rs.at[b])
        p_ref[b, core] = p_ref[b, core] + c_ref[b]
        to_heads(p_ref.at[b, core], x_ref.at[b], x_ss.at[b], x_rs.at[b], across).start()

    def cross_y(i, p_ref, c_ref, x_ref, y_ref, c_rs, x_rs, y_ss, y_rs):
        b = 4 + i
        take(c_ref.at[b], c_rs.at[b])
        take(x_ref.at[i], x_rs.at[i])
        p_ref[b, core] = p_ref[b, core] + c_ref[b] + x_ref[i]
        off = 3 - i
        if off:
            to_heads(
                p_ref.at[b, core], y_ref.at[off - 1], y_ss.at[off - 1], y_rs.at[off - 1], along_y(off)
            ).start()

    score_block(0)
    pl.semaphore_wait(barrier, 20)
    send_stats(0)

    def main_step(b, carry):
        score_block(b)
        send_stats(b)

        @pl.when(b >= LAG)
        def _():
            target_block(b - LAG)

        @pl.when(b >= LAG + 1)
        def _():
            cross_x(b - LAG - 1, tp_ref, tc_ref, tx_ref, tc_rs, tx_ss, tx_rs)

        return carry

    lax.fori_loop(1, 8, main_step, 0)

    sub = lax.broadcasted_iota(jnp.int32, (8, 128), 0)
    is_ref[...] = jnp.zeros((16, 2048), F32)

    def index_step(g, carry):
        rows = pl.ds(pl.multiple_of(g * 256, 256), 256)
        lg_ref[rows, :] = lax.dot_general(iq[rows, :], ik[...], NT, preferred_element_type=F32)

        def one(j, inner):
            q = g * 4 + j
            qrows = pl.ds(pl.multiple_of(q * 64, 64), 64)
            w = wcol_ref[qrows, :]
            eight = pl.ds(pl.multiple_of((q // 8) * 8, 8), 8)
            for t in range(16):
                got = jnp.sum(jnp.maximum(lg_ref[qrows, lanes(t)], 0.0) * w, axis=0, keepdims=True)
                is_ref[eight, lanes(t)] = jnp.where(
                    sub == q % 8, jnp.broadcast_to(got, (8, 128)), is_ref[eight, lanes(t)]
                )
            return inner

        lax.fori_loop(0, 4, one, 0)

        @pl.when(g < LAG)
        def _():
            target_block(8 - LAG + g)

        return carry

    lax.fori_loop(0, 4, index_step, 0)

    row = lax.broadcasted_iota(jnp.int32, (16, 128), 0)
    posr = jnp.zeros((16, 128), jnp.int32)
    klr = jnp.zeros((16, 128), F32)
    for q in range(16):
        posr = jnp.where(row == q, pos_s[h * 16 + q] - key_first, posr)
        klr = jnp.where(row == q, kl_s[q], klr)
    top = jnp.full((16, 128), FLOOR, F32)
    for t in range(16):
        v = jnp.where(lane + t * 128 <= posr, is_ref[:, lanes(t)], MASKED)
        is_ref[:, lanes(t)] = v
        top = jnp.maximum(top, v)
    im = jnp.broadcast_to(jnp.max(top, axis=1, keepdims=True), (16, 128))
    total = jnp.zeros((16, 128), F32)
    for t in range(16):
        e = jnp.exp(is_ref[:, lanes(t)] - im)
        total = total + e
        ie_ref[:, lanes(t)] = e
    il = jnp.broadcast_to(jnp.sum(total, axis=1, keepdims=True), (16, 128))
    ist_mine[...] = jnp.where(lane == 0, im, il)
    for r in range(1, 16):
        to_keys(ist_mine, ist_all.at[r - 1], ist_ss, ist_rs, (k + r) % 16).start()

    for i in range(4):
        cross_y(i, tp_ref, tc_ref, tx_ref, ty_ref, tc_rs, tx_rs, ty_ss, ty_rs)

    take(ist_all, ist_rs)
    ms = [jnp.broadcast_to(ist_all[r][:, 0:1], (16, 128)) for r in range(15)]
    top = im
    for m in ms:
        top = jnp.maximum(top, m)
    share = jnp.exp(im - top)
    total = il * share
    for r in range(15):
        total = total + jnp.broadcast_to(ist_all[r][:, 1:2], (16, 128)) * jnp.exp(ms[r] - top)
    share = share / total

    for j in range(3):
        take(ty_ref.at[j], ty_rs.at[j])
    for t in range(16):
        target = tp_ref[7, core, :, lanes(t)]
        for j in range(3):
            target = target + ty_ref[j, :, lanes(t)]
        delta = klr * (ie_ref[:, lanes(t)] * share - target)
        for q in range(16):
            d_ref[q, :, lanes(t)] = jnp.broadcast_to(delta[q:q + 1, :], (8, 128))

    def back_step(n, carry):
        g = (z // 2 + 1 + n) % 4
        wgc_ref[...] = jnp.zeros((128, 128), F32)

        def one(j, inner):
            q = g * 4 + j
            qrows = pl.ds(pl.multiple_of(q * 64, 64), 64)
            w = wcol_ref[qrows, :]
            acc = jnp.zeros((64, 128), F32)
            for t in range(16):
                d = jnp.concatenate([d_ref[q, :, lanes(t)]] * 8, axis=0)
                v = lg_ref[qrows, lanes(t)]
                sl_ref[qrows, lanes(t)] = jnp.where(v > 0.0, d * w, 0.0).astype(BF16)
                acc = acc + jnp.maximum(v, 0.0) * d
            col = jnp.broadcast_to(jnp.sum(acc, axis=1, keepdims=True), (64, 128))
            at = (j // 2) * 8 + j % 2
            wgc_ref[0:64, :] = jnp.where(lane == at, col, wgc_ref[0:64, :])
            return inner

        lax.fori_loop(0, 4, one, 0)
        turned = jnp.transpose(wgc_ref[...])
        rows = pl.ds(pl.multiple_of(g * 256, 256), 256)
        got = jnp.dot(sl_ref[rows, :], ik[...], preferred_element_type=F32)
        for j in range(2):
            blk = g * 2 + j
            qg_part[blk, 0:128, :] = got[j * 128:(j + 1) * 128, :]
            qg_part[blk, 128:136, :] = turned[j * 8:(j + 1) * 8, :]
            r = (blk - z + 8) % 8

            @pl.when(r > 0)
            def _():
                to_keys(
                    qg_part.at[blk], qg_recv.at[r - 1], qg_ss.at[r - 1], qg_rs.at[r - 1], blk * 2 + xh
                ).start()

        return carry

    lax.fori_loop(0, 4, back_step, 0)

    def key_step(b, carry):
        cols = pl.ds(pl.multiple_of(chip(b) * 256, 256), 256)
        got = jnp.dot(iqt_ref[...], sl_ref[:, cols], preferred_element_type=F32)
        kp_ref[b, 0] = got[:, 0:128]
        kp_ref[b, 1] = got[:, 128:256]
        to_heads(kp_ref.at[b, 1 - core], kc_ref.at[b], kc_ss.at[b], kc_rs.at[b], partner).start()

        @pl.when((b >= 1) & (b < 5))
        def _():
            cross_x(b - 1, kp_ref, kc_ref, kx_ref, kc_rs, kx_ss, kx_rs)

        return carry

    lax.fori_loop(0, 8, key_step, 0)

    for j in range(7):
        take(qg_recv.at[j], qg_rs.at[j])
    acc = qg_part[z]
    for j in range(7):
        acc = acc + qg_recv[j]
    qg_part[z] = acc
    to_keys(qg_part.at[z], qg_xh, xh_ss, xh_rs, z * 2 + (1 - xh)).start()

    for i in range(4):
        cross_y(i, kp_ref, kc_ref, kx_ref, ky_ref, kc_rs, kx_rs, ky_ss, ky_rs)

    take(qg_xh, xh_rs)
    qg_all[z] = qg_part[z] + qg_xh[...]
    for r in range(1, 8):
        to_keys(
            qg_all.at[z], qg_all.at[z], qa_ss.at[r - 1], qa_rs.at[r - 1], ((z + r) % 8) * 2 + xh
        ).start()

    for j in range(3):
        take(ky_ref.at[j], ky_rs.at[j])
    shard = kp_ref[7, core]
    for j in range(3):
        shard = shard + ky_ref[j]
    kg_all[h] = jnp.transpose(shard)

    def pass_on(s, peer, n):
        to_heads(kg_all.at[s], kg_all.at[s], ka_ss.at[n], ka_rs.at[s], peer).start()

    for off in (1, 2, 3):
        pass_on(h, along_y(off), off - 1)
    pass_on(h, across, 3)
    pass_on(h, partner, 4)
    for off in (1, 3, 2):
        s = along_y(off)
        take(kg_all.at[s], ka_rs.at[s])
        pass_on(s, across, 4 + off)
        pass_on(s, partner, 7 + off)
    for off in (0, 1, 3, 2):
        s = (1 - x) * 8 + ((y + off) % 4) * 2 + core
        take(kg_all.at[s], ka_rs.at[s])
        pass_on(s, partner, 11 + off)

    for r in range(1, 8):
        take(qg_all.at[(z - r + 8) % 8], qa_rs.at[r - 1])
    for i in range(8):
        qg_out[i * 128:(i + 1) * 128, :] = qg_all[i, 0:128, :]
        wg_out[i * 2:(i + 1) * 2, :] = qg_all[i, 128:130, 0:64]
    for c in range(8):
        s = c * 2 + (1 - core)
        take(kg_all.at[s], ka_rs.at[s])
    for s in range(16):
        kg_out[s * 128:(s + 1) * 128, :] = kg_all[s]

    for b in range(8):
        take(stat_all.at[b], stat_ss.at[b])
        take(tc_ref.at[b], tc_ss.at[b])
        take(kc_ref.at[b], kc_ss.at[b])
    take(ist_all, ist_ss)
    for b in range(4):
        take(tx_ref.at[b], tx_ss.at[b])
        take(kx_ref.at[b], kx_ss.at[b])
    for j in range(3):
        take(ty_ref.at[j], ty_ss.at[j])
        take(ky_ref.at[j], ky_ss.at[j])
    for j in range(7):
        take(qg_recv.at[j], qg_ss.at[j])
        take(qg_all.at[j], qa_ss.at[j])
    take(qg_xh, xh_ss)
    for n in range(15):
        take(kg_all.at[n], ka_ss.at[n])


def shards(main_query, latent_keys, index_query, index_keys, index_weight, query_pos, kl_weight):
    vmem = pl.BlockSpec(memory_space=pltpu.VMEM)
    smem = pl.BlockSpec(memory_space=pltpu.SMEM)
    dma = pltpu.SemaphoreType.DMA
    query_grad, key_grad, weight_grad = pl.pallas_call(
        fused,
        out_shape=(
            jax.ShapeDtypeStruct((1024, 128), F32),
            jax.ShapeDtypeStruct((2048, 128), F32),
            jax.ShapeDtypeStruct((16, 64), F32),
        ),
        in_specs=[smem, smem] + [vmem] * 5,
        out_specs=(vmem, vmem, vmem),
        scratch_shapes=[
            pltpu.VMEM((256, 2048), F32),
            pltpu.VMEM((2048, 2048), BF16),
            pltpu.VMEM((256, 128), F32),
            pltpu.VMEM((8, 2, 256), F32),
            pltpu.VMEM((8, 15, 2, 256), F32),
            pltpu.VMEM((8, 2, 16, 2048), F32),
            pltpu.VMEM((8, 16, 2048), F32),
            pltpu.VMEM((4, 16, 2048), F32),
            pltpu.VMEM((3, 16, 2048), F32),
            pltpu.VMEM((1024, 2048), F32),
            pltpu.VMEM((128, 128), F32),
            pltpu.VMEM((1024, 128), F32),
            pltpu.VMEM((128, 1024), BF16),
            pltpu.VMEM((16, 2048), F32),
            pltpu.VMEM((16, 2048), F32),
            pltpu.VMEM((16, 128), F32),
            pltpu.VMEM((15, 16, 128), F32),
            pltpu.VMEM((16, 8, 2048), F32),
            pltpu.VMEM((1024, 2048), BF16),
            pltpu.VMEM((128, 128), F32),
            pltpu.VMEM((8, 136, 128), F32),
            pltpu.VMEM((7, 136, 128), F32),
            pltpu.VMEM((136, 128), F32),
            pltpu.VMEM((8, 136, 128), F32),
            pltpu.VMEM((8, 2, 128, 128), F32),
            pltpu.VMEM((8, 128, 128), F32),
            pltpu.VMEM((4, 128, 128), F32),
            pltpu.VMEM((3, 128, 128), F32),
            pltpu.VMEM((16, 128, 128), F32),
            dma((8,)), dma((8,)), dma, dma,
            dma((8,)), dma((8,)), dma((4,)), dma((4,)), dma((3,)), dma((3,)),
            dma((7,)), dma((7,)), dma, dma, dma((7,)), dma((7,)),
            dma((8,)), dma((8,)), dma((4,)), dma((4,)), dma((3,)), dma((3,)),
            dma((15,)), dma((16,)),
        ],
        compiler_params=pltpu.CompilerParams(
            collective_id=0, has_side_effects=True, vmem_limit_bytes=60 * 1024 * 1024
        ),
        name="fused_indexer_step",
    )(
        query_pos,
        kl_weight,
        main_query.reshape(2048, 576),
        latent_keys,
        index_query.reshape(1024, 128),
        index_keys,
        index_weight,
    )
    return query_grad.reshape(16, 64, 128), key_grad, weight_grad


def solution(mesh):
    placed = (
        P(None, "heads", None),
        P("keys", None),
        P("heads", None, None),
        P("keys", None),
        P("heads", None),
        P(),
        P("heads"),
    )
    return jax.shard_map(
        shards,
        mesh=mesh,
        in_specs=placed,
        out_specs=(P("heads", None, None), P("keys", None), P("heads", None)),
        check_vma=False,
    )
```

time: 566 us -> 93.7 us (0.17)
  waiting for transfers between devices: 379 us -> 0 us
  blocking collectives: 108 us -> 0 us
  Pallas kernels: 0 us -> 80.4 us
  matrix products: 35.3 us -> 0 us
  other arithmetic: 21.1 us -> 0 us
  between operations: 13.9 us -> 0.66 us
    psum x3 -> x0, waiting for transfers between devices: 379 us -> none  [the longest x1 140 us: shards(): summed = lax.psum(partial_value, 'heads')]
    pallas_call x0 -> x1, Pallas kernels: none -> 80.4 us  [shards(): pl.pallas_call(fused, out_shape=(jax.ShapeDtypeStruct((1024, 128), F32),...]
    psum x2 -> x0, blocking collectives: 68.1 us -> none  [the longest x1 36.5 us: shards(): query_grad, weight_grad = lax.psum((query_grad, weight_grad), 'keys')]
    pmax x1 -> x0, blocking collectives: 39.7 us -> none  [shards(): main_maxima, index_maxima = lax.pmax((main_local, index_local), 'keys')]
    dot_general x6 -> x0, matrix products: 35.3 us -> none  [the longest x2 15 us: contract_last(): lax.dot_general(left_side, right_side, (((1,), (1,)), ((), ())), preferre...]
    reduce_sum x3 -> x0, other arithmetic: 18.8 us -> none  [the longest x1 10.2 us: shards(): partial_value = jnp.sum(main_probs, axis=1)]
    unnamed x20 -> x9, local copies, waits for them, and re-layouts: 7.41 us -> 12.4 us
  transfers between devices with their start and end apart: 3 -> 0, of which waited for: 3 -> 0; matrix products, arithmetic and copies ran while one was open for 2% -> 0% of each run, Pallas kernels for 0% -> 0%
where the time goes in v1:
time: 93.7 us; the launch traced here: 93.5 us
  Pallas kernels  80.4 us (86%)
  local copies, waits for them, and re-layouts  12.4 us (13%)
    pallas_call x1, Pallas kernels, shards(): pl.pallas_call(fused, out_shape=(jax.ShapeDtypeStruct((1024, 128), F32),...  80.4 us
    unnamed x9, local copies, waits for them, and re-layouts  12.4 us

profile of v1, /device:TPU:1, one launch (start us, length us, event | category | flops | bytes accessed | tf_op | source)
XLA Modules:
  0.0 93.5 jit_solution(6123359206487898668)
XLA Ops:
  0.6 0.0 copy-start
  0.6 5.0 %copy.10 = bf16[256,8,576]{2,1,0:T(8,128)(2,1)} copy(bf16[256,8,576]{0,2,1:T(8,128)(2,1)} %param.7) | data formatting | bytes 4718592 | tf_op args[0]
  5.7 0.0 copy-done
  5.7 2.6 %copy.11.lk = bf16[2048,576]{1,0:T(8,128)(2,1)} copy(bf16[2048,576]{0,1:T(8,128)(2,1)S(1)} %copy-done) | data formatting | bytes 4718592 | tf_op args[1]
  8.3 80.4 %fused_indexer_step.1 = (f32[1024,128]{1,0:T(8,128)}, f32[2048,128]{1,0:T(8,128)}, f32[16,64]{1,0:T(8,128)}) custom-call(s32[256]{0:T(256)} %pos_s.1, f32[16]{0:T(128)} %kl_s.1, bf16[2048,576]{1,0:T(8,128)(2,1)} %bitcast.3, bf16[2048,576]{1,0:T(8,128)(2,1)} %copy.11.lk, bf16[1024,128]{1,0:T(8,128)(2,1)} %bitcast.5, bf16[2048,128]{1,0:T(8,128)(2,1)} %ik.1, ...), custom_call_target="tpu_custom_call" | custom-call | tf_op jit(solution)/shard_map/fused_indexer_step/pallas_call | solution.py:383
  88.7 0.0 copy-start.1
  88.7 1.9 %copy.15 = f32[16,64,128]{2,1,0:T(8,128)} copy(f32[16,64,128]{2,1,0:T(8,128)} %bitcast.4) | data formatting | bytes 1048576
  90.6 2.3 %copy.16 = f32[2048,128]{1,0:T(8,128)} copy(f32[2048,128]{1,0:T(8,128)} %get-tuple-element.13) | data formatting | bytes 2097152
  92.9 0.0 copy-done.1
  92.9 0.6 copy.17
Async XLA Ops:
  0.6 5.1 %copy-start = (bf16[2048,576]{0,1:T(8,128)(2,1)S(1)}, bf16[2048,576]{0,1:T(8,128)(2,1)}, u32[]{:S(2)}) copy-start(bf16[2048,576]{0,1:T(8,128)(2,1)} %param.8) | copy-start | bytes 7077892
  88.7 4.2 %copy-start.1 = (f32[16,64]{1,0:T(8,128)S(1)}, f32[16,64]{1,0:T(8,128)}, u32[]{:S(2)}) copy-start(f32[16,64]{1,0:T(8,128)} %get-tuple-element.14) | copy-start | bytes 12292

commit v2 on v1

--- a/solution.py
+++ b/solution.py
@@ -7,6 +7,7 @@
 
 H = 128
 SCALE = 192.0 ** (-0.5)
+SCALE2 = SCALE * 1.4426950408889634
 MASKED = -1e30
 FLOOR = -1e29
 MESH = pl.DeviceIdType.MESH
@@ -21,18 +22,23 @@
 
 
 def fused(
-    pos_s, kl_s, mq, lk, iq, ik, iw,
-    qg_out, kg_out, wg_out,
-    s_ref, e_ref, st_ref, stat_mine, stat_all,
+    pos_s, kl_s, mqt_hbm, lkt_hbm, iq, ik, iw,
+    qg_all, kg_all,
+    mqt, lkt, mq_ref, posb_ref,
+    s_a, s_b, e_ref, st_ref, stat_mine, stat_all,
     tp_ref, tc_ref, tx_ref, ty_ref,
     lg_ref, wpad_ref, wcol_ref, iqt_ref, is_ref, ie_ref, ist_mine, ist_all, d_ref,
-    sl_ref, wgc_ref, qg_part, qg_recv, qg_xh, qg_all,
-    kp_ref, kc_ref, kx_ref, ky_ref, kg_all,
+    sl_ref, wgc_ref, qg_part, qg_recv, qg_xh,
+    kp_ref, kc_ref, kx_ref, ky_ref,
+    mq_in, lk_in,
     stat_ss, stat_rs, ist_ss, ist_rs,
     tc_ss, tc_rs, tx_ss, tx_rs, ty_ss, ty_rs,
     qg_ss, qg_rs, xh_ss, xh_rs, qa_ss, qa_rs,
     kc_ss, kc_rs, kx_ss, kx_rs, ky_ss, ky_rs, ka_ss, ka_rs,
 ):
+    for i in range(8):
+        pltpu.make_async_copy(mqt_hbm.at[i], mqt.at[i], mq_in.at[i]).start()
+    pltpu.make_async_copy(lkt_hbm, lkt, lk_in).start()
     h = lax.axis_index("heads")
     k = lax.axis_index("keys")
     core, y, x = h % 2, (h // 2) % 4, h // 8
@@ -54,6 +60,7 @@
         pl.semaphore_signal(barrier, inc=1, device_id={"heads": peer}, device_id_type=MESH)
 
     lane = lax.broadcasted_iota(jnp.int32, (1, 128), 1)
+    sub = lax.broadcasted_iota(jnp.int32, (8, 128), 0)
 
     wpad_ref[...] = jnp.zeros((128, 128), F32)
     wpad_ref[0:16, 0:64] = iw[...]
@@ -61,7 +68,20 @@
     for q in range(16):
         wcol_ref[q * 64:(q + 1) * 64, :] = jnp.broadcast_to(wturned[0:64, q:q + 1], (64, 128))
     for i in range(8):
-        iqt_ref[:, lanes(i)] = jnp.transpose(iq[lanes(i), :].astype(F32)).astype(BF16)
+        iqt_ref[:, lanes(i)] = jnp.transpose(iq[lanes(i), :].astype(F32) * wcol_ref[lanes(i), :]).astype(BF16)
+
+    unit = lax.broadcasted_iota(jnp.int32, (256, 256), 0) == lax.broadcasted_iota(jnp.int32, (256, 256), 1)
+    unit = jnp.where(unit, 1.0, 0.0).astype(BF16)
+
+    def turn(i, carry):
+        pltpu.make_async_copy(mqt_hbm.at[i], mqt.at[i], mq_in.at[i]).wait()
+        got = lax.dot_general(unit, mqt[i], NT, preferred_element_type=F32).astype(BF16)
+        for c in range(8):
+            mq_ref[c, i] = got[c * 32:(c + 1) * 32, :]
+        return carry
+
+    lax.fori_loop(0, 8, turn, 0)
+    pltpu.make_async_copy(lkt_hbm, lkt, lk_in).wait()
 
     def to_heads(src, dst, ss, rs, peer):
         return pltpu.make_async_remote_copy(
@@ -78,37 +98,40 @@
     def take(ref, sem):
         pltpu.make_async_copy(ref, ref, sem).wait()
 
-    def score_block(b):
-        c = chip(b)
-        r0 = pl.multiple_of(c * 256, 256)
-        s_ref[...] = lax.dot_general(mq[pl.ds(r0, 256), :], lk[...], NT, preferred_element_type=F32)
-
-        def piece(i, carry):
-            rows = pl.ds(pl.multiple_of(i * 64, 64), 64)
-            posv = jnp.concatenate(
-                [jnp.full((8, 128), pos_s[c * 32 + i * 8 + j] - key_first, jnp.int32) for j in range(8)],
-                axis=0,
-            )
-            top = jnp.full((64, 128), FLOOR, F32)
-            for t in range(16):
-                v = jnp.where(lane + t * 128 <= posv, s_ref[rows, lanes(t)], MASKED)
-                s_ref[rows, lanes(t)] = v
-                top = jnp.maximum(top, v)
-            mcol = jnp.broadcast_to(jnp.max(top, axis=1, keepdims=True), (64, 128))
-            total = jnp.zeros((64, 128), F32)
-            erows = pl.ds(pl.multiple_of(r0 + i * 64, 64), 64)
-            for t in range(16):
-                e = jnp.exp((s_ref[rows, lanes(t)] - mcol) * SCALE)
-                total = total + e
-                e_ref[erows, lanes(t)] = e.astype(BF16)
-            lcol = jnp.broadcast_to(jnp.sum(total, axis=1, keepdims=True), (64, 128))
-            st_ref[rows, :] = jnp.where(lane == 0, mcol, lcol)
-            return carry
-
-        lax.fori_loop(0, 4, piece, 0)
+    def score_quarter(b, i, s_ref):
+        cols = pl.ds(pl.multiple_of(i * 512, 512), 512)
+        s_ref[:, cols] = jnp.dot(
+            mq_ref[chip(b)].reshape(256, 576), lkt[:, cols], preferred_element_type=F32
+        )
+
+    def soft_piece(b, i, s_ref):
+        r0 = pl.multiple_of(chip(b) * 256, 256)
+        rows = pl.ds(pl.multiple_of(i * 64, 64), 64)
+        reach = jnp.concatenate([posb_ref[...]] * 2, axis=0)
+        top = jnp.full((64, 128), FLOOR, F32)
+        for t in range(16):
+            v = jnp.where(reach >= t * 128, s_ref[rows, lanes(t)], MASKED)
+            s_ref[rows, lanes(t)] = v
+            top = jnp.maximum(top, v)
+        mcol = jnp.broadcast_to(jnp.max(top, axis=1, keepdims=True), (64, 128))
+        total = jnp.zeros((64, 128), F32)
+        erows = pl.ds(pl.multiple_of(r0 + i * 64, 64), 64)
+        for t in range(16):
+            e = jnp.exp2((s_ref[rows, lanes(t)] - mcol) * SCALE2)
+            total = total + e
+            e_ref[erows, lanes(t)] = e.astype(BF16)
+        lcol = jnp.broadcast_to(jnp.sum(total, axis=1, keepdims=True), (64, 128))
+        st_ref[rows, :] = jnp.where(lane == 0, mcol, lcol)
+
+    def reach_of(b):
+        for n in range(4):
+            got = jnp.zeros((8, 128), jnp.int32)
+            for j in range(8):
+                got = jnp.where(sub == j, pos_s[chip(b) * 32 + n * 8 + j] - key_first, got)
+            posb_ref[n * 8:(n + 1) * 8, :] = got - lane
+
+    def send_stats(b):
         stat_mine[b] = jnp.transpose(st_ref[...])[0:2, :]
-
-    def send_stats(b):
         for r in range(1, 16):
             to_keys(stat_mine.at[b], stat_all.at[b, r - 1], stat_ss.at[b], stat_rs.at[b], (k + r) % 16).start()
 
@@ -128,7 +151,7 @@
         w = share / (total * float(H))
         high = w.astype(BF16).astype(F32)
         low = w - high
-        mine_of = lax.broadcasted_iota(jnp.int32, (32, 256), 1) // 8 == lax.broadcasted_iota(
+        mine_of = lax.broadcasted_iota(jnp.int32, (32, 256), 1) % 32 == lax.broadcasted_iota(
             jnp.int32, (32, 256), 0
         )
         a = jnp.concatenate([jnp.where(mine_of, high, 0.0), jnp.where(mine_of, low, 0.0)], axis=0)
@@ -155,12 +178,22 @@
                 p_ref.at[b, core], y_ref.at[off - 1], y_ss.at[off - 1], y_rs.at[off - 1], along_y(off)
             ).start()
 
-    score_block(0)
+    def first(i, carry):
+        score_quarter(0, i, s_a)
+        return carry
+
+    lax.fori_loop(0, 4, first, 0)
     pl.semaphore_wait(barrier, 20)
-    send_stats(0)
-
-    def main_step(b, carry):
-        score_block(b)
+
+    def one_block(b, s_now, s_next):
+        reach_of(b)
+
+        def quarter(i, carry):
+            score_quarter(jnp.minimum(b + 1, 7), i, s_next)
+            soft_piece(b, i, s_now)
+            return carry
+
+        lax.fori_loop(0, 4, quarter, 0)
         send_stats(b)
 
         @pl.when(b >= LAG)
@@ -171,30 +204,32 @@
         def _():
             cross_x(b - LAG - 1, tp_ref, tc_ref, tx_ref, tc_rs, tx_ss, tx_rs)
 
+    def two_blocks(n, carry):
+        one_block(n * 2, s_a, s_b)
+        one_block(n * 2 + 1, s_b, s_a)
         return carry
 
-    lax.fori_loop(1, 8, main_step, 0)
-
-    sub = lax.broadcasted_iota(jnp.int32, (8, 128), 0)
-    is_ref[...] = jnp.zeros((16, 2048), F32)
+    lax.fori_loop(0, 4, two_blocks, 0)
 
     def index_step(g, carry):
         rows = pl.ds(pl.multiple_of(g * 256, 256), 256)
-        lg_ref[rows, :] = lax.dot_general(iq[rows, :], ik[...], NT, preferred_element_type=F32)
-
-        def one(j, inner):
-            q = g * 4 + j
-            qrows = pl.ds(pl.multiple_of(q * 64, 64), 64)
-            w = wcol_ref[qrows, :]
-            eight = pl.ds(pl.multiple_of((q // 8) * 8, 8), 8)
-            for t in range(16):
-                got = jnp.sum(jnp.maximum(lg_ref[qrows, lanes(t)], 0.0) * w, axis=0, keepdims=True)
-                is_ref[eight, lanes(t)] = jnp.where(
-                    sub == q % 8, jnp.broadcast_to(got, (8, 128)), is_ref[eight, lanes(t)]
-                )
+
+        def quarter(i, inner):
+            got = lax.dot_general(
+                iq[rows, :], ik[pl.ds(pl.multiple_of(i * 512, 512), 512), :], NT, preferred_element_type=F32
+            )
+            for t in range(4):
+                cols = pl.ds(pl.multiple_of(i * 512 + t * 128, 128), 128)
+                for j in range(4):
+                    qrows = pl.ds(pl.multiple_of(g * 256 + j * 64, 64), 64)
+                    v = got[j * 64:(j + 1) * 64, lanes(t)]
+                    lg_ref[qrows, cols] = v.astype(BF16)
+                    is_ref[g, j:j + 1, cols] = jnp.sum(
+                        jnp.maximum(v, 0.0) * wcol_ref[qrows, :], axis=0, keepdims=True
+                    )
             return inner
 
-        lax.fori_loop(0, 4, one, 0)
+        lax.fori_loop(0, 4, quarter, 0)
 
         @pl.when(g < LAG)
         def _():
@@ -212,13 +247,14 @@
         klr = jnp.where(row == q, kl_s[q], klr)
     top = jnp.full((16, 128), FLOOR, F32)
     for t in range(16):
-        v = jnp.where(lane + t * 128 <= posr, is_ref[:, lanes(t)], MASKED)
-        is_ref[:, lanes(t)] = v
+        v = jnp.concatenate([is_ref[g, 0:4, lanes(t)] for g in range(4)], axis=0)
+        v = jnp.where(lane + t * 128 <= posr, v, MASKED)
+        ie_ref[:, lanes(t)] = v
         top = jnp.maximum(top, v)
     im = jnp.broadcast_to(jnp.max(top, axis=1, keepdims=True), (16, 128))
     total = jnp.zeros((16, 128), F32)
     for t in range(16):
-        e = jnp.exp(is_ref[:, lanes(t)] - im)
+        e = jnp.exp(ie_ref[:, lanes(t)] - im)
         total = total + e
         ie_ref[:, lanes(t)] = e
     il = jnp.broadcast_to(jnp.sum(total, axis=1, keepdims=True), (16, 128))
@@ -248,31 +284,26 @@
             target = target + ty_ref[j, :, lanes(t)]
         delta = klr * (ie_ref[:, lanes(t)] * share - target)
         for q in range(16):
-            d_ref[q, :, lanes(t)] = jnp.broadcast_to(delta[q:q + 1, :], (8, 128))
+            d_ref[q, :, lanes(t)] = jnp.broadcast_to(delta[q:q + 1, :], (16, 128)).astype(BF16)
 
     def back_step(n, carry):
         g = (z // 2 + 1 + n) % 4
+        rows = pl.ds(pl.multiple_of(g * 256, 256), 256)
+        for j in range(4):
+            qrows = pl.ds(pl.multiple_of(g * 256 + j * 64, 64), 64)
+            for t in range(16):
+                d = jnp.concatenate([d_ref[g * 4 + j, :, lanes(t)]] * 4, axis=0)
+                sl_ref[qrows, lanes(t)] = jnp.where(lg_ref[qrows, lanes(t)] > 0, d, jnp.zeros((64, 128), BF16))
+        got = jnp.dot(sl_ref[rows, :], ik[...], preferred_element_type=F32)
+        along = jnp.sum(got * iq[rows, :].astype(F32), axis=1, keepdims=True)
         wgc_ref[...] = jnp.zeros((128, 128), F32)
-
-        def one(j, inner):
-            q = g * 4 + j
-            qrows = pl.ds(pl.multiple_of(q * 64, 64), 64)
-            w = wcol_ref[qrows, :]
-            acc = jnp.zeros((64, 128), F32)
-            for t in range(16):
-                d = jnp.concatenate([d_ref[q, :, lanes(t)]] * 8, axis=0)
-                v = lg_ref[qrows, lanes(t)]
-                sl_ref[qrows, lanes(t)] = jnp.where(v > 0.0, d * w, 0.0).astype(BF16)
-                acc = acc + jnp.maximum(v, 0.0) * d
-            col = jnp.broadcast_to(jnp.sum(acc, axis=1, keepdims=True), (64, 128))
+        columns = jnp.zeros((64, 128), F32)
+        for j in range(4):
             at = (j // 2) * 8 + j % 2
-            wgc_ref[0:64, :] = jnp.where(lane == at, col, wgc_ref[0:64, :])
-            return inner
-
-        lax.fori_loop(0, 4, one, 0)
+            columns = jnp.where(lane == at, jnp.broadcast_to(along[j * 64:(j + 1) * 64], (64, 128)), columns)
+        wgc_ref[0:64, :] = columns
         turned = jnp.transpose(wgc_ref[...])
-        rows = pl.ds(pl.multiple_of(g * 256, 256), 256)
-        got = jnp.dot(sl_ref[rows, :], ik[...], preferred_element_type=F32)
+        got = got * wcol_ref[rows, :]
         for j in range(2):
             blk = g * 2 + j
             qg_part[blk, 0:128, :] = got[j * 128:(j + 1) * 128, :]
@@ -348,14 +379,9 @@
 
     for r in range(1, 8):
         take(qg_all.at[(z - r + 8) % 8], qa_rs.at[r - 1])
-    for i in range(8):
-        qg_out[i * 128:(i + 1) * 128, :] = qg_all[i, 0:128, :]
-        wg_out[i * 2:(i + 1) * 2, :] = qg_all[i, 128:130, 0:64]
     for c in range(8):
         s = c * 2 + (1 - core)
         take(kg_all.at[s], ka_rs.at[s])
-    for s in range(16):
-        kg_out[s * 128:(s + 1) * 128, :] = kg_all[s]
 
     for b in range(8):
         take(stat_all.at[b], stat_ss.at[b])
@@ -376,20 +402,33 @@
         take(kg_all.at[n], ka_ss.at[n])
 
 
+def finish(qg_all, kg_all, qg_out, kg_out, wg_out):
+    for i in range(8):
+        qg_out[i * 128:(i + 1) * 128, :] = qg_all[i, 0:128, :]
+        wg_out[i * 2:(i + 1) * 2, :] = qg_all[i, 128:130, 0:64]
+    for i in range(16):
+        kg_out[i * 128:(i + 1) * 128, :] = kg_all[i]
+
+
 def shards(main_query, latent_keys, index_query, index_keys, index_weight, query_pos, kl_weight):
     vmem = pl.BlockSpec(memory_space=pltpu.VMEM)
     smem = pl.BlockSpec(memory_space=pltpu.SMEM)
+    hbm = pl.BlockSpec(memory_space=pl.ANY)
     dma = pltpu.SemaphoreType.DMA
-    query_grad, key_grad, weight_grad = pl.pallas_call(
+    query_blocks, key_blocks = pl.pallas_call(
         fused,
         out_shape=(
-            jax.ShapeDtypeStruct((1024, 128), F32),
-            jax.ShapeDtypeStruct((2048, 128), F32),
-            jax.ShapeDtypeStruct((16, 64), F32),
+            jax.ShapeDtypeStruct((8, 136, 128), F32),
+            jax.ShapeDtypeStruct((16, 128, 128), F32),
         ),
-        in_specs=[smem, smem] + [vmem] * 5,
-        out_specs=(vmem, vmem, vmem),
+        in_specs=[smem, smem, hbm, hbm, vmem, vmem, vmem],
+        out_specs=(vmem, vmem),
         scratch_shapes=[
+            pltpu.VMEM((8, 576, 256), BF16),
+            pltpu.VMEM((576, 2048), BF16),
+            pltpu.VMEM((8, 8, 32, 576), BF16),
+            pltpu.VMEM((32, 128), jnp.int32),
+            pltpu.VMEM((256, 2048), F32),
             pltpu.VMEM((256, 2048), F32),
             pltpu.VMEM((2048, 2048), BF16),
             pltpu.VMEM((256, 128), F32),
@@ -399,26 +438,25 @@
             pltpu.VMEM((8, 16, 2048), F32),
             pltpu.VMEM((4, 16, 2048), F32),
             pltpu.VMEM((3, 16, 2048), F32),
-            pltpu.VMEM((1024, 2048), F32),
+            pltpu.VMEM((1024, 2048), BF16),
             pltpu.VMEM((128, 128), F32),
             pltpu.VMEM((1024, 128), F32),
             pltpu.VMEM((128, 1024), BF16),
-            pltpu.VMEM((16, 2048), F32),
+            pltpu.VMEM((4, 8, 2048), F32),
             pltpu.VMEM((16, 2048), F32),
             pltpu.VMEM((16, 128), F32),
             pltpu.VMEM((15, 16, 128), F32),
-            pltpu.VMEM((16, 8, 2048), F32),
+            pltpu.VMEM((16, 16, 2048), BF16),
             pltpu.VMEM((1024, 2048), BF16),
             pltpu.VMEM((128, 128), F32),
             pltpu.VMEM((8, 136, 128), F32),
             pltpu.VMEM((7, 136, 128), F32),
             pltpu.VMEM((136, 128), F32),
-            pltpu.VMEM((8, 136, 128), F32),
             pltpu.VMEM((8, 2, 128, 128), F32),
             pltpu.VMEM((8, 128, 128), F32),
             pltpu.VMEM((4, 128, 128), F32),
             pltpu.VMEM((3, 128, 128), F32),
-            pltpu.VMEM((16, 128, 128), F32),
+            dma((8,)), dma,
             dma((8,)), dma((8,)), dma, dma,
             dma((8,)), dma((8,)), dma((4,)), dma((4,)), dma((3,)), dma((3,)),
             dma((7,)), dma((7,)), dma, dma, dma((7,)), dma((7,)),
@@ -432,12 +470,23 @@
     )(
         query_pos,
         kl_weight,
-        main_query.reshape(2048, 576),
-        latent_keys,
+        jnp.transpose(main_query, (1, 2, 0)),
+        jnp.transpose(latent_keys, (1, 0)),
         index_query.reshape(1024, 128),
         index_keys,
         index_weight,
     )
+    query_grad, key_grad, weight_grad = pl.pallas_call(
+        finish,
+        out_shape=(
+            jax.ShapeDtypeStruct((1024, 128), F32),
+            jax.ShapeDtypeStruct((2048, 128), F32),
+            jax.ShapeDtypeStruct((16, 64), F32),
+        ),
+        in_specs=[vmem, vmem],
+        out_specs=(vmem, vmem, vmem),
+        name="finish",
+    )(query_blocks, key_blocks)
     return query_grad.reshape(16, 64, 128), key_grad, weight_grad
 
 

time: 93.7 us -> 81.7 us (0.87)
  local copies, waits for them, and re-layouts: 12.4 us -> 0 us
    unnamed x9 -> x0, local copies, waits for them, and re-layouts: 12.4 us -> none
    pallas_call x1 -> x2, Pallas kernels: 80.4 us -> 80.9 us  [the longest x1 78.3 us: shards(): pl.pallas_call(fused, out_shape=(jax.ShapeDtypeStruct((8, 136, 128), F32)...]
where the time goes in v2:
time: 81.7 us; the launch traced here: 81.6 us
  Pallas kernels  80.9 us (99%)
    pallas_call x1, Pallas kernels, shards(): pl.pallas_call(fused, out_shape=(jax.ShapeDtypeStruct((8, 136, 128), F32)...  78.3 us
    pallas_call x1, Pallas kernels, shards(): pl.pallas_call(finish, out_shape=(jax.ShapeDtypeStruct((1024, 128), F32),...  2.61 us

profile of v2, /device:TPU:1, one launch (start us, length us, event | category | flops | bytes accessed | tf_op | source)
XLA Modules:
  0.0 81.6 jit_solution(13278713702853179801)
XLA Ops:
  0.6 78.3 %fused_indexer_step.1 = (f32[8,136,128]{2,1,0:T(8,128)}, f32[16,128,128]{2,1,0:T(8,128)}) custom-call(s32[256]{0:T(256)} %pos_s.1, f32[16]{0:T(128)} %kl_s.1, bf16[8,576,256]{2,1,0:T(8,128)(2,1)} %bitcast.4, bf16[576,2048]{1,0:T(8,128)(2,1)} %bitcast.5, bf16[1024,128]{1,0:T(8,128)(2,1)} %bitcast.6, bf16[2048,128]{1,0:T(8,128)(2,1)} %ik.1, f32[16,64]{1,0:T(8,128)} %iw.1), custom_call_target="tpu_custom_call" | custom-call | tf_op jit(solution)/shard_map/fused_indexer_step/pallas_call | solution.py:418
  79.0 2.6 %finish.1 = (f32[1024,128]{1,0:T(8,128)}, f32[2048,128]{1,0:T(8,128)}, f32[16,64]{1,0:T(8,128)}) custom-call(f32[8,136,128]{2,1,0:T(8,128)} %get-tuple-element.8.qg_all, f32[16,128,128]{2,1,0:T(8,128)} %get-tuple-element.9.kg_all), custom_call_target="tpu_custom_call" | custom-call | tf_op jit(solution)/shard_map/finish/pallas_call | solution.py:479

commit v3 on v2

--- a/solution.py
+++ b/solution.py
@@ -1,3 +1,5 @@
+import functools
+
 import jax
 import jax.numpy as jnp
 from jax import lax
@@ -24,21 +26,22 @@
 def fused(
     pos_s, kl_s, mqt_hbm, lkt_hbm, iq, ik, iw,
     qg_all, kg_all,
-    mqt, lkt, mq_ref, posb_ref,
-    s_a, s_b, e_ref, st_ref, stat_mine, stat_all,
+    mqt, lkt_in, posb_ref,
+    s_a, s_b, st_ref, stat_mine, stat_all,
     tp_ref, tc_ref, tx_ref, ty_ref,
-    lg_ref, wpad_ref, wcol_ref, iqt_ref, is_ref, ie_ref, ist_mine, ist_all, d_ref,
-    sl_ref, wgc_ref, qg_part, qg_recv, qg_xh,
+    wpad_ref, wcol_ref, is_ref, ie_ref, ist_mine, ist_all,
+    wgc_ref, qg_part, qg_recv, qg_four, qg_xh,
     kp_ref, kc_ref, kx_ref, ky_ref,
     mq_in, lk_in,
     stat_ss, stat_rs, ist_ss, ist_rs,
     tc_ss, tc_rs, tx_ss, tx_rs, ty_ss, ty_rs,
     qg_ss, qg_rs, xh_ss, xh_rs, qa_ss, qa_rs,
     kc_ss, kc_rs, kx_ss, kx_rs, ky_ss, ky_rs, ka_ss, ka_rs,
+    lkt, mq_ref, e_ref, lg_ref, iqt_ref, ikc, d_ref, sl_ref,
 ):
     for i in range(8):
         pltpu.make_async_copy(mqt_hbm.at[i], mqt.at[i], mq_in.at[i]).start()
-    pltpu.make_async_copy(lkt_hbm, lkt, lk_in).start()
+    pltpu.make_async_copy(lkt_hbm, lkt_in, lk_in).start()
     h = lax.axis_index("heads")
     k = lax.axis_index("keys")
     core, y, x = h % 2, (h // 2) % 4, h // 8
@@ -62,14 +65,6 @@
     lane = lax.broadcasted_iota(jnp.int32, (1, 128), 1)
     sub = lax.broadcasted_iota(jnp.int32, (8, 128), 0)
 
-    wpad_ref[...] = jnp.zeros((128, 128), F32)
-    wpad_ref[0:16, 0:64] = iw[...]
-    wturned = jnp.transpose(wpad_ref[...])
-    for q in range(16):
-        wcol_ref[q * 64:(q + 1) * 64, :] = jnp.broadcast_to(wturned[0:64, q:q + 1], (64, 128))
-    for i in range(8):
-        iqt_ref[:, lanes(i)] = jnp.transpose(iq[lanes(i), :].astype(F32) * wcol_ref[lanes(i), :]).astype(BF16)
-
     unit = lax.broadcasted_iota(jnp.int32, (256, 256), 0) == lax.broadcasted_iota(jnp.int32, (256, 256), 1)
     unit = jnp.where(unit, 1.0, 0.0).astype(BF16)
 
@@ -81,7 +76,15 @@
         return carry
 
     lax.fori_loop(0, 8, turn, 0)
-    pltpu.make_async_copy(lkt_hbm, lkt, lk_in).wait()
+    pltpu.make_async_copy(lkt_hbm, lkt_in, lk_in).wait()
+
+    def settle(i, carry):
+        rows = pl.ds(pl.multiple_of(i * 64, 64), 64)
+        lkt[rows, :] = lkt_in[rows, :]
+        return carry
+
+    lax.fori_loop(0, 9, settle, 0)
+    ikc[...] = ik[...]
 
     def to_heads(src, dst, ss, rs, peer):
         return pltpu.make_async_remote_copy(
@@ -188,12 +191,9 @@
     def one_block(b, s_now, s_next):
         reach_of(b)
 
-        def quarter(i, carry):
+        for i in range(4):
             score_quarter(jnp.minimum(b + 1, 7), i, s_next)
             soft_piece(b, i, s_now)
-            return carry
-
-        lax.fori_loop(0, 4, quarter, 0)
         send_stats(b)
 
         @pl.when(b >= LAG)
@@ -211,17 +211,25 @@
 
     lax.fori_loop(0, 4, two_blocks, 0)
 
+    wpad_ref[...] = jnp.zeros((128, 128), F32)
+    wpad_ref[0:16, 0:64] = iw[...]
+    wturned = jnp.transpose(wpad_ref[...])
+    for q in range(16):
+        wcol_ref[q * 64:(q + 1) * 64, :] = jnp.broadcast_to(wturned[0:64, q:q + 1], (64, 128))
+    for i in range(8):
+        iqt_ref[:, lanes(i)] = jnp.transpose(iq[lanes(i), :].astype(F32) * wcol_ref[lanes(i), :]).astype(BF16)
+
     def index_step(g, carry):
         rows = pl.ds(pl.multiple_of(g * 256, 256), 256)
 
-        def quarter(i, inner):
+        def part(i, inner):
             got = lax.dot_general(
-                iq[rows, :], ik[pl.ds(pl.multiple_of(i * 512, 512), 512), :], NT, preferred_element_type=F32
+                iq[rows, :], ikc[pl.ds(pl.multiple_of(i * 256, 256), 256), :], NT, preferred_element_type=F32
             )
-            for t in range(4):
-                cols = pl.ds(pl.multiple_of(i * 512 + t * 128, 128), 128)
-                for j in range(4):
-                    qrows = pl.ds(pl.multiple_of(g * 256 + j * 64, 64), 64)
+            for j in range(4):
+                qrows = pl.ds(pl.multiple_of(g * 256 + j * 64, 64), 64)
+                for t in range(2):
+                    cols = pl.ds(pl.multiple_of(i * 256 + t * 128, 128), 128)
                     v = got[j * 64:(j + 1) * 64, lanes(t)]
                     lg_ref[qrows, cols] = v.astype(BF16)
                     is_ref[g, j:j + 1, cols] = jnp.sum(
@@ -229,7 +237,7 @@
                     )
             return inner
 
-        lax.fori_loop(0, 4, quarter, 0)
+        lax.fori_loop(0, 8, part, 0)
 
         @pl.when(g < LAG)
         def _():
@@ -286,39 +294,63 @@
         for q in range(16):
             d_ref[q, :, lanes(t)] = jnp.broadcast_to(delta[q:q + 1, :], (16, 128)).astype(BF16)
 
-    def back_step(n, carry):
-        g = (z // 2 + 1 + n) % 4
-        rows = pl.ds(pl.multiple_of(g * 256, 256), 256)
-        for j in range(4):
-            qrows = pl.ds(pl.multiple_of(g * 256 + j * 64, 64), 64)
-            for t in range(16):
-                d = jnp.concatenate([d_ref[g * 4 + j, :, lanes(t)]] * 4, axis=0)
-                sl_ref[qrows, lanes(t)] = jnp.where(lg_ref[qrows, lanes(t)] > 0, d, jnp.zeros((64, 128), BF16))
-        got = jnp.dot(sl_ref[rows, :], ik[...], preferred_element_type=F32)
-        along = jnp.sum(got * iq[rows, :].astype(F32), axis=1, keepdims=True)
-        wgc_ref[...] = jnp.zeros((128, 128), F32)
+    def z_peer(off):
+        return ((z + off) % 8) * 2 + xh
+
+    def back_step(offsets):
+        picked = []
+        for off in offsets:
+            q0 = ((z + off) % 8) * 2
+            for j in range(2):
+                qrows = pl.ds(pl.multiple_of((q0 + j) * 64, 64), 64)
+                for t in range(16):
+                    d = jnp.concatenate([d_ref[q0 + j, :, lanes(t)]] * 4, axis=0)
+                    sl_ref[qrows, lanes(t)] = jnp.where(
+                        lg_ref[qrows, lanes(t)] > 0, d, jnp.zeros((64, 128), BF16)
+                    )
+            picked.append(pl.ds(pl.multiple_of(q0 * 64, 128), 128))
+        gate = jnp.concatenate([sl_ref[rows, :] for rows in picked], axis=0)
+        both = jnp.dot(gate, ikc[...], preferred_element_type=F32)
         columns = jnp.zeros((64, 128), F32)
-        for j in range(4):
-            at = (j // 2) * 8 + j % 2
-            columns = jnp.where(lane == at, jnp.broadcast_to(along[j * 64:(j + 1) * 64], (64, 128)), columns)
+        for n, (off, rows) in enumerate(zip(offsets, picked)):
+            got = both[n * 128:(n + 1) * 128, :]
+            along = jnp.sum(got * iq[rows, :].astype(F32), axis=1, keepdims=True)
+            for j in range(2):
+                columns = jnp.where(
+                    lane == n * 8 + j, jnp.broadcast_to(along[j * 64:(j + 1) * 64], (64, 128)), columns
+                )
+            qg_part[off, 0:128, :] = got * wcol_ref[rows, :]
         wgc_ref[0:64, :] = columns
         turned = jnp.transpose(wgc_ref[...])
-        got = got * wcol_ref[rows, :]
-        for j in range(2):
-            blk = g * 2 + j
-            qg_part[blk, 0:128, :] = got[j * 128:(j + 1) * 128, :]
-            qg_part[blk, 128:136, :] = turned[j * 8:(j + 1) * 8, :]
-            r = (blk - z + 8) % 8
-
-            @pl.when(r > 0)
-            def _():
-                to_keys(
-                    qg_part.at[blk], qg_recv.at[r - 1], qg_ss.at[r - 1], qg_rs.at[r - 1], blk * 2 + xh
-                ).start()
-
-        return carry
-
-    lax.fori_loop(0, 4, back_step, 0)
+        for n, off in enumerate(offsets):
+            qg_part[off, 128:136, :] = turned[n * 8:(n + 1) * 8, :]
+
+    def z_send(src, dst, n, off):
+        to_keys(src, dst, qg_ss.at[n], qg_rs.at[n], z_peer(off)).start()
+
+    wgc_ref[...] = jnp.zeros((128, 128), F32)
+    back_step((4, 3))
+    z_send(qg_part.at[4, 0:72], qg_four.at[0:72], 0, 2)
+    z_send(qg_part.at[4, 72:136], qg_four.at[72:136], 1, 6)
+    z_send(qg_part.at[3], qg_recv.at[0], 2, 1)
+    back_step((5, 2))
+    z_send(qg_part.at[5], qg_recv.at[1], 3, 7)
+    back_step((6, 1))
+    z_send(qg_part.at[1], qg_recv.at[2], 4, 1)
+    back_step((7, 0))
+    z_send(qg_part.at[7], qg_recv.at[3], 5, 7)
+
+    def z_join():
+        take(qg_recv.at[0], qg_rs.at[2])
+        take(qg_four.at[0:72], qg_rs.at[0])
+        qg_part[2, 0:72, :] = qg_part[2, 0:72, :] + qg_recv[0, 0:72, :] + qg_four[0:72, :]
+        qg_part[2, 72:136, :] = qg_part[2, 72:136, :] + qg_recv[0, 72:136, :]
+        z_send(qg_part.at[2], qg_recv.at[4], 6, 2)
+        take(qg_recv.at[1], qg_rs.at[3])
+        take(qg_four.at[72:136], qg_rs.at[1])
+        qg_part[6, 0:72, :] = qg_part[6, 0:72, :] + qg_recv[1, 0:72, :]
+        qg_part[6, 72:136, :] = qg_part[6, 72:136, :] + qg_recv[1, 72:136, :] + qg_four[72:136, :]
+        z_send(qg_part.at[6], qg_recv.at[5], 7, 6)
 
     def key_step(b, carry):
         cols = pl.ds(pl.multiple_of(chip(b) * 256, 256), 256)
@@ -327,6 +359,10 @@
         kp_ref[b, 1] = got[:, 128:256]
         to_heads(kp_ref.at[b, 1 - core], kc_ref.at[b], kc_ss.at[b], kc_rs.at[b], partner).start()
 
+        @pl.when(b == 2)
+        def _():
+            z_join()
+
         @pl.when((b >= 1) & (b < 5))
         def _():
             cross_x(b - 1, kp_ref, kc_ref, kx_ref, kc_rs, kx_ss, kx_rs)
@@ -335,23 +371,13 @@
 
     lax.fori_loop(0, 8, key_step, 0)
 
-    for j in range(7):
-        take(qg_recv.at[j], qg_rs.at[j])
-    acc = qg_part[z]
-    for j in range(7):
-        acc = acc + qg_recv[j]
-    qg_part[z] = acc
-    to_keys(qg_part.at[z], qg_xh, xh_ss, xh_rs, z * 2 + (1 - xh)).start()
-
     for i in range(4):
         cross_y(i, kp_ref, kc_ref, kx_ref, ky_ref, kc_rs, kx_rs, ky_ss, ky_rs)
 
-    take(qg_xh, xh_rs)
-    qg_all[z] = qg_part[z] + qg_xh[...]
-    for r in range(1, 8):
-        to_keys(
-            qg_all.at[z], qg_all.at[z], qa_ss.at[r - 1], qa_rs.at[r - 1], ((z + r) % 8) * 2 + xh
-        ).start()
+    for j in range(4):
+        take(qg_recv.at[2 + j], qg_rs.at[4 + j])
+    qg_part[0] = qg_part[0] + (qg_recv[2] + qg_recv[3]) + (qg_recv[4] + qg_recv[5])
+    to_keys(qg_part.at[0], qg_xh, xh_ss, xh_rs, z * 2 + (1 - xh)).start()
 
     for j in range(3):
         take(ky_ref.at[j], ky_rs.at[j])
@@ -367,18 +393,43 @@
         pass_on(h, along_y(off), off - 1)
     pass_on(h, across, 3)
     pass_on(h, partner, 4)
+
+    def z_back(off_from, part, n, off):
+        ref = qg_all.at[(z + off_from) % 8, part]
+        to_keys(ref, ref, qa_ss.at[n], qa_rs.at[n], z_peer(off)).start()
+
+    def z_take(off_from, part, n):
+        take(qg_all.at[(z + off_from) % 8, part], qa_rs.at[n])
+
+    whole, front, rear = slice(0, 136), slice(0, 72), slice(72, 136)
+    take(qg_xh, xh_rs)
+    qg_all[z] = qg_part[0] + qg_xh[...]
+    z_back(0, whole, 0, 2)
+    z_back(0, whole, 1, 6)
+    z_back(0, whole, 2, 1)
+    z_back(0, whole, 3, 7)
     for off in (1, 3, 2):
         s = along_y(off)
         take(kg_all.at[s], ka_rs.at[s])
         pass_on(s, across, 4 + off)
         pass_on(s, partner, 7 + off)
+    z_take(6, whole, 0)
+    z_back(6, front, 4, 2)
+    z_back(6, whole, 5, 1)
+    z_take(2, whole, 1)
+    z_back(2, rear, 6, 6)
+    z_back(2, whole, 7, 7)
     for off in (0, 1, 3, 2):
         s = (1 - x) * 8 + ((y + off) % 4) * 2 + core
         take(kg_all.at[s], ka_rs.at[s])
         pass_on(s, partner, 11 + off)
 
-    for r in range(1, 8):
-        take(qg_all.at[(z - r + 8) % 8], qa_rs.at[r - 1])
+    z_take(7, whole, 2)
+    z_take(1, whole, 3)
+    z_take(4, front, 4)
+    z_take(5, whole, 5)
+    z_take(4, rear, 6)
+    z_take(3, whole, 7)
     for c in range(8):
         s = c * 2 + (1 - core)
         take(kg_all.at[s], ka_rs.at[s])
@@ -394,12 +445,29 @@
     for j in range(3):
         take(ty_ref.at[j], ty_ss.at[j])
         take(ky_ref.at[j], ky_ss.at[j])
-    for j in range(7):
-        take(qg_recv.at[j], qg_ss.at[j])
-        take(qg_all.at[j], qa_ss.at[j])
+    take(qg_four.at[0:72], qg_ss.at[0])
+    take(qg_four.at[72:136], qg_ss.at[1])
+    for j in range(6):
+        take(qg_recv.at[j], qg_ss.at[2 + j])
+    for n, part in enumerate((whole, whole, whole, whole, front, whole, rear, whole)):
+        take(qg_all.at[0, part], qa_ss.at[n])
     take(qg_xh, xh_ss)
     for n in range(15):
         take(kg_all.at[n], ka_ss.at[n])
+
+
+def scoped(*refs):
+    pl.run_scoped(
+        functools.partial(fused, *refs),
+        pltpu.VMEM((576, 2048), BF16),
+        pltpu.VMEM((8, 8, 32, 576), BF16),
+        pltpu.VMEM((2048, 2048), BF16),
+        pltpu.VMEM((1024, 2048), BF16),
+        pltpu.VMEM((128, 1024), BF16),
+        pltpu.VMEM((2048, 128), BF16),
+        pltpu.VMEM((16, 16, 2048), BF16),
+        pltpu.VMEM((1024, 2048), BF16),
+    )
 
 
 def finish(qg_all, kg_all, qg_out, kg_out, wg_out):
@@ -416,7 +484,7 @@
     hbm = pl.BlockSpec(memory_space=pl.ANY)
     dma = pltpu.SemaphoreType.DMA
     query_blocks, key_blocks = pl.pallas_call(
-        fused,
+        scoped,
         out_shape=(
             jax.ShapeDtypeStruct((8, 136, 128), F32),
             jax.ShapeDtypeStruct((16, 128, 128), F32),
@@ -426,11 +494,9 @@
         scratch_shapes=[
             pltpu.VMEM((8, 576, 256), BF16),
             pltpu.VMEM((576, 2048), BF16),
-            pltpu.VMEM((8, 8, 32, 576), BF16),
             pltpu.VMEM((32, 128), jnp.int32),
             pltpu.VMEM((256, 2048), F32),
             pltpu.VMEM((256, 2048), F32),
-            pltpu.VMEM((2048, 2048), BF16),
             pltpu.VMEM((256, 128), F32),
             pltpu.VMEM((8, 2, 256), F32),
             pltpu.VMEM((8, 15, 2, 256), F32),
@@ -438,19 +504,16 @@
             pltpu.VMEM((8, 16, 2048), F32),
             pltpu.VMEM((4, 16, 2048), F32),
             pltpu.VMEM((3, 16, 2048), F32),
-            pltpu.VMEM((1024, 2048), BF16),
             pltpu.VMEM((128, 128), F32),
             pltpu.VMEM((1024, 128), F32),
-            pltpu.VMEM((128, 1024), BF16),
             pltpu.VMEM((4, 8, 2048), F32),
             pltpu.VMEM((16, 2048), F32),
             pltpu.VMEM((16, 128), F32),
             pltpu.VMEM((15, 16, 128), F32),
-            pltpu.VMEM((16, 16, 2048), BF16),
-            pltpu.VMEM((1024, 2048), BF16),
             pltpu.VMEM((128, 128), F32),
             pltpu.VMEM((8, 136, 128), F32),
-            pltpu.VMEM((7, 136, 128), F32),
+            pltpu.VMEM((6, 136, 128), F32),
+            pltpu.VMEM((136, 128), F32),
             pltpu.VMEM((136, 128), F32),
             pltpu.VMEM((8, 2, 128, 128), F32),
             pltpu.VMEM((8, 128, 128), F32),
@@ -459,7 +522,7 @@
             dma((8,)), dma,
             dma((8,)), dma((8,)), dma, dma,
             dma((8,)), dma((8,)), dma((4,)), dma((4,)), dma((3,)), dma((3,)),
-            dma((7,)), dma((7,)), dma, dma, dma((7,)), dma((7,)),
+            dma((8,)), dma((8,)), dma, dma, dma((8,)), dma((8,)),
             dma((8,)), dma((8,)), dma((4,)), dma((4,)), dma((3,)), dma((3,)),
             dma((15,)), dma((16,)),
         ],

time: 81.7 us -> 76 us (0.930)
  Pallas kernels: 80.9 us -> 75.2 us
    pallas_call x1, Pallas kernels: 78.3 us -> 72.6 us  [shards(): pl.pallas_call(scoped, out_shape=(jax.ShapeDtypeStruct((8, 136, 128), F32...]
where the time goes in v3:
time: 76 us; the launch traced here: 75.9 us
  Pallas kernels  75.2 us (99%)
    pallas_call x1, Pallas kernels, shards(): pl.pallas_call(scoped, out_shape=(jax.ShapeDtypeStruct((8, 136, 128), F32...  72.6 us
    pallas_call x1, Pallas kernels, shards(): pl.pallas_call(finish, out_shape=(jax.ShapeDtypeStruct((1024, 128), F32),...  2.61 us

profile of v3, /device:TPU:1, one launch (start us, length us, event | category | flops | bytes accessed | tf_op | source)
XLA Modules:
  0.0 75.9 jit_solution(6770806582549881249)
XLA Ops:
  0.6 72.6 %fused_indexer_step.1 = (f32[8,136,128]{2,1,0:T(8,128)}, f32[16,128,128]{2,1,0:T(8,128)}) custom-call(s32[256]{0:T(256)} %refs_0_.1, f32[16]{0:T(128)} %refs_1_.1, bf16[8,576,256]{2,1,0:T(8,128)(2,1)} %bitcast.4, bf16[576,2048]{1,0:T(8,128)(2,1)} %bitcast.5, bf16[1024,128]{1,0:T(8,128)(2,1)} %bitcast.6, bf16[2048,128]{1,0:T(8,128)(2,1)} %refs_5_.1, ...), custom_call_target="tpu_custom_call" | custom-call | tf_op jit(solution)/shard_map/fused_indexer_step/pallas_call | solution.py:486
  73.3 2.6 %finish.1 = (f32[1024,128]{1,0:T(8,128)}, f32[2048,128]{1,0:T(8,128)}, f32[16,64]{1,0:T(8,128)}) custom-call(f32[8,136,128]{2,1,0:T(8,128)} %get-tuple-element.8.qg_all, f32[16,128,128]{2,1,0:T(8,128)} %get-tuple-element.9.kg_all), custom_call_target="tpu_custom_call" | custom-call | tf_op jit(solution)/shard_map/finish/pallas_call | solution.py:542

commit v4 on v3

--- a/solution.py
+++ b/solution.py
@@ -12,6 +12,7 @@
 SCALE2 = SCALE * 1.4426950408889634
 MASKED = -1e30
 FLOOR = -1e29
+HUGE = 1e30
 MESH = pl.DeviceIdType.MESH
 LAG = 3
 NT = (((1,), (1,)), ((), ()))
@@ -65,6 +66,39 @@
     lane = lax.broadcasted_iota(jnp.int32, (1, 128), 1)
     sub = lax.broadcasted_iota(jnp.int32, (8, 128), 0)
 
+    ikc[...] = ik[...]
+
+    wpad_ref[...] = jnp.zeros((128, 128), F32)
+    wpad_ref[0:16, 0:64] = iw[...]
+    wturned = jnp.transpose(wpad_ref[...])
+    for q in range(16):
+        wcol_ref[q * 64:(q + 1) * 64, :] = jnp.broadcast_to(wturned[0:64, q:q + 1], (64, 128))
+    for i in range(8):
+        iqt_ref[:, lanes(i)] = jnp.transpose(iq[lanes(i), :].astype(F32) * wcol_ref[lanes(i), :]).astype(BF16)
+
+    def index_step(g, carry):
+        rows = pl.ds(pl.multiple_of(g * 256, 256), 256)
+
+        def part(i, inner):
+            got = lax.dot_general(
+                iq[rows, :], ikc[pl.ds(pl.multiple_of(i * 256, 256), 256), :], NT, preferred_element_type=F32
+            )
+            for j in range(4):
+                qrows = pl.ds(pl.multiple_of(g * 256 + j * 64, 64), 64)
+                for t in range(2):
+                    cols = pl.ds(pl.multiple_of(i * 256 + t * 128, 128), 128)
+                    v = got[j * 64:(j + 1) * 64, lanes(t)]
+                    lg_ref[qrows, cols] = v.astype(BF16)
+                    is_ref[g, j:j + 1, cols] = jnp.sum(
+                        jnp.maximum(v, 0.0) * wcol_ref[qrows, :], axis=0, keepdims=True
+                    )
+            return inner
+
+        lax.fori_loop(0, 8, part, 0)
+        return carry
+
+    lax.fori_loop(0, 2, index_step, 0)
+
     unit = lax.broadcasted_iota(jnp.int32, (256, 256), 0) == lax.broadcasted_iota(jnp.int32, (256, 256), 1)
     unit = jnp.where(unit, 1.0, 0.0).astype(BF16)
 
@@ -84,7 +118,6 @@
         return carry
 
     lax.fori_loop(0, 9, settle, 0)
-    ikc[...] = ik[...]
 
     def to_heads(src, dst, ss, rs, peer):
         return pltpu.make_async_remote_copy(
@@ -113,7 +146,7 @@
         reach = jnp.concatenate([posb_ref[...]] * 2, axis=0)
         top = jnp.full((64, 128), FLOOR, F32)
         for t in range(16):
-            v = jnp.where(reach >= t * 128, s_ref[rows, lanes(t)], MASKED)
+            v = jnp.minimum(s_ref[rows, lanes(t)], reach + (0.5 - t * 128) * HUGE)
             s_ref[rows, lanes(t)] = v
             top = jnp.maximum(top, v)
         mcol = jnp.broadcast_to(jnp.max(top, axis=1, keepdims=True), (64, 128))
@@ -131,7 +164,7 @@
             got = jnp.zeros((8, 128), jnp.int32)
             for j in range(8):
                 got = jnp.where(sub == j, pos_s[chip(b) * 32 + n * 8 + j] - key_first, got)
-            posb_ref[n * 8:(n + 1) * 8, :] = got - lane
+            posb_ref[n * 8:(n + 1) * 8, :] = (got - lane).astype(F32) * HUGE
 
     def send_stats(b):
         stat_mine[b] = jnp.transpose(st_ref[...])[0:2, :]
@@ -192,8 +225,8 @@
         reach_of(b)
 
         for i in range(4):
+            soft_piece(b, i, s_now)
             score_quarter(jnp.minimum(b + 1, 7), i, s_next)
-            soft_piece(b, i, s_now)
         send_stats(b)
 
         @pl.when(b >= LAG)
@@ -211,41 +244,22 @@
 
     lax.fori_loop(0, 4, two_blocks, 0)
 
-    wpad_ref[...] = jnp.zeros((128, 128), F32)
-    wpad_ref[0:16, 0:64] = iw[...]
-    wturned = jnp.transpose(wpad_ref[...])
-    for q in range(16):
-        wcol_ref[q * 64:(q + 1) * 64, :] = jnp.broadcast_to(wturned[0:64, q:q + 1], (64, 128))
-    for i in range(8):
-        iqt_ref[:, lanes(i)] = jnp.transpose(iq[lanes(i), :].astype(F32) * wcol_ref[lanes(i), :]).astype(BF16)
-
-    def index_step(g, carry):
-        rows = pl.ds(pl.multiple_of(g * 256, 256), 256)
-
-        def part(i, inner):
-            got = lax.dot_general(
-                iq[rows, :], ikc[pl.ds(pl.multiple_of(i * 256, 256), 256), :], NT, preferred_element_type=F32
-            )
-            for j in range(4):
-                qrows = pl.ds(pl.multiple_of(g * 256 + j * 64, 64), 64)
-                for t in range(2):
-                    cols = pl.ds(pl.multiple_of(i * 256 + t * 128, 128), 128)
-                    v = got[j * 64:(j + 1) * 64, lanes(t)]
-                    lg_ref[qrows, cols] = v.astype(BF16)
-                    is_ref[g, j:j + 1, cols] = jnp.sum(
-                        jnp.maximum(v, 0.0) * wcol_ref[qrows, :], axis=0, keepdims=True
-                    )
-            return inner
-
-        lax.fori_loop(0, 8, part, 0)
-
-        @pl.when(g < LAG)
+    def own_chip(i):
+        cross_y(i, tp_ref, tc_ref, tx_ref, ty_ref, tc_rs, tx_rs, ty_ss, ty_rs)
+
+    target_block(5)
+
+    def index_rest(g, carry):
+        index_step(g, carry)
+
+        @pl.when(g == 2)
         def _():
-            target_block(8 - LAG + g)
-
-        return carry
-
-    lax.fori_loop(0, 4, index_step, 0)
+            own_chip(0)
+
+        return carry
+
+    lax.fori_loop(2, 4, index_rest, 0)
+    own_chip(1)
 
     row = lax.broadcasted_iota(jnp.int32, (16, 128), 0)
     posr = jnp.zeros((16, 128), jnp.int32)
@@ -270,8 +284,10 @@
     for r in range(1, 16):
         to_keys(ist_mine, ist_all.at[r - 1], ist_ss, ist_rs, (k + r) % 16).start()
 
-    for i in range(4):
-        cross_y(i, tp_ref, tc_ref, tx_ref, ty_ref, tc_rs, tx_rs, ty_ss, ty_rs)
+    target_block(6)
+    target_block(7)
+    own_chip(2)
+    own_chip(3)
 
     take(ist_all, ist_rs)
     ms = [jnp.broadcast_to(ist_all[r][:, 0:1], (16, 128)) for r in range(15)]
@@ -359,17 +375,14 @@
         kp_ref[b, 1] = got[:, 128:256]
         to_heads(kp_ref.at[b, 1 - core], kc_ref.at[b], kc_ss.at[b], kc_rs.at[b], partner).start()
 
-        @pl.when(b == 2)
+        @pl.when(b >= 4)
         def _():
-            z_join()
-
-        @pl.when((b >= 1) & (b < 5))
-        def _():
-            cross_x(b - 1, kp_ref, kc_ref, kx_ref, kc_rs, kx_ss, kx_rs)
+            cross_x(b - 4, kp_ref, kc_ref, kx_ref, kc_rs, kx_ss, kx_rs)
 
         return carry
 
     lax.fori_loop(0, 8, key_step, 0)
+    z_join()
 
     for i in range(4):
         cross_y(i, kp_ref, kc_ref, kx_ref, ky_ref, kc_rs, kx_rs, ky_ss, ky_rs)
@@ -471,11 +484,16 @@
 
 
 def finish(qg_all, kg_all, qg_out, kg_out, wg_out):
-    for i in range(8):
+    for i in range(2):
         qg_out[i * 128:(i + 1) * 128, :] = qg_all[i, 0:128, :]
-        wg_out[i * 2:(i + 1) * 2, :] = qg_all[i, 128:130, 0:64]
-    for i in range(16):
+    for i in range(4):
         kg_out[i * 128:(i + 1) * 128, :] = kg_all[i]
+    for n in range(4):
+
+        @pl.when(pl.program_id(0) == n)
+        def _():
+            for i in range(2):
+                wg_out[n * 4 + i * 2:n * 4 + (i + 1) * 2, :] = qg_all[i, 128:130, 0:64]
 
 
 def shards(main_query, latent_keys, index_query, index_keys, index_weight, query_pos, kl_weight):
@@ -494,7 +512,7 @@
         scratch_shapes=[
             pltpu.VMEM((8, 576, 256), BF16),
             pltpu.VMEM((576, 2048), BF16),
-            pltpu.VMEM((32, 128), jnp.int32),
+            pltpu.VMEM((32, 128), F32),
             pltpu.VMEM((256, 2048), F32),
             pltpu.VMEM((256, 2048), F32),
             pltpu.VMEM((256, 128), F32),
@@ -546,8 +564,16 @@
             jax.ShapeDtypeStruct((2048, 128), F32),
             jax.ShapeDtypeStruct((16, 64), F32),
         ),
-        in_specs=[vmem, vmem],
-        out_specs=(vmem, vmem, vmem),
+        grid=(4,),
+        in_specs=[
+            pl.BlockSpec((2, 136, 128), lambda n: (n, 0, 0)),
+            pl.BlockSpec((4, 128, 128), lambda n: (n, 0, 0)),
+        ],
+        out_specs=(
+            pl.BlockSpec((256, 128), lambda n: (n, 0)),
+            pl.BlockSpec((512, 128), lambda n: (n, 0)),
+            pl.BlockSpec((16, 64), lambda n: (0, 0)),
+        ),
         name="finish",
     )(query_blocks, key_blocks)
     return query_grad.reshape(16, 64, 128), key_grad, weight_grad

time: 76 us -> 76.2 us (level); the launches traced: 75.9 us -> 75.2 us
    pallas_call x1, Pallas kernels: 72.6 us -> 70.9 us  [shards(): pl.pallas_call(scoped, out_shape=(jax.ShapeDtypeStruct((8, 136, 128), F32...]
    pallas_call x1, Pallas kernels: 2.61 us -> 3.65 us  [shards(): pl.pallas_call(finish, out_shape=(jax.ShapeDtypeStruct((1024, 128), F32),...]
where the time goes in v4:
time: 76.2 us; the launch traced here: 75.2 us
  Pallas kernels  74.5 us (98%)
    pallas_call x1, Pallas kernels, shards(): pl.pallas_call(scoped, out_shape=(jax.ShapeDtypeStruct((8, 136, 128), F32...  70.9 us
    pallas_call x1, Pallas kernels, shards(): pl.pallas_call(finish, out_shape=(jax.ShapeDtypeStruct((1024, 128), F32),...  3.65 us

profile of v4, /device:TPU:1, one launch (start us, length us, event | category | flops | bytes accessed | tf_op | source)
XLA Modules:
  0.0 75.2 jit_solution(5269032203094605764)
XLA Ops:
  0.6 70.9 %fused_indexer_step.1 = (f32[8,136,128]{2,1,0:T(8,128)}, f32[16,128,128]{2,1,0:T(8,128)}) custom-call(s32[256]{0:T(256)} %refs_0_.1, f32[16]{0:T(128)} %refs_1_.1, bf16[8,576,256]{2,1,0:T(8,128)(2,1)} %bitcast.4, bf16[576,2048]{1,0:T(8,128)(2,1)} %bitcast.5, bf16[1024,128]{1,0:T(8,128)(2,1)} %bitcast.6, bf16[2048,128]{1,0:T(8,128)(2,1)} %refs_5_.1, ...), custom_call_target="tpu_custom_call" | custom-call | tf_op jit(solution)/shard_map/fused_indexer_step/pallas_call | solution.py:504
  71.5 3.7 %finish.1 = (f32[1024,128]{1,0:T(8,128)}, f32[2048,128]{1,0:T(8,128)}, f32[16,64]{1,0:T(8,128)}) custom-call(f32[8,136,128]{2,1,0:T(8,128)} %get-tuple-element.8.qg_all, f32[16,128,128]{2,1,0:T(8,128)} %get-tuple-element.9.kg_all), custom_call_target="tpu_custom_call" | custom-call | tf_op jit(solution)/shard_map/finish/pallas_call | solution.py:560

commit v5 on v4

--- a/solution.py
+++ b/solution.py
@@ -38,7 +38,7 @@
     tc_ss, tc_rs, tx_ss, tx_rs, ty_ss, ty_rs,
     qg_ss, qg_rs, xh_ss, xh_rs, qa_ss, qa_rs,
     kc_ss, kc_rs, kx_ss, kx_rs, ky_ss, ky_rs, ka_ss, ka_rs,
-    lkt, mq_ref, e_ref, lg_ref, iqt_ref, ikc, d_ref, sl_ref,
+    lkt, mq_ref, e_ref, lg_ref, iqt_ref, ikc, d_ref, sl_ref, ikt,
 ):
     for i in range(8):
         pltpu.make_async_copy(mqt_hbm.at[i], mqt.at[i], mq_in.at[i]).start()
@@ -73,31 +73,20 @@
     wturned = jnp.transpose(wpad_ref[...])
     for q in range(16):
         wcol_ref[q * 64:(q + 1) * 64, :] = jnp.broadcast_to(wturned[0:64, q:q + 1], (64, 128))
-    for i in range(8):
-        iqt_ref[:, lanes(i)] = jnp.transpose(iq[lanes(i), :].astype(F32) * wcol_ref[lanes(i), :]).astype(BF16)
-
-    def index_step(g, carry):
+    def index_part(g, i):
         rows = pl.ds(pl.multiple_of(g * 256, 256), 256)
-
-        def part(i, inner):
-            got = lax.dot_general(
-                iq[rows, :], ikc[pl.ds(pl.multiple_of(i * 256, 256), 256), :], NT, preferred_element_type=F32
-            )
-            for j in range(4):
-                qrows = pl.ds(pl.multiple_of(g * 256 + j * 64, 64), 64)
-                for t in range(2):
-                    cols = pl.ds(pl.multiple_of(i * 256 + t * 128, 128), 128)
-                    v = got[j * 64:(j + 1) * 64, lanes(t)]
-                    lg_ref[qrows, cols] = v.astype(BF16)
-                    is_ref[g, j:j + 1, cols] = jnp.sum(
-                        jnp.maximum(v, 0.0) * wcol_ref[qrows, :], axis=0, keepdims=True
-                    )
-            return inner
-
-        lax.fori_loop(0, 8, part, 0)
-        return carry
-
-    lax.fori_loop(0, 2, index_step, 0)
+        got = lax.dot_general(
+            iq[rows, :], ikc[pl.ds(pl.multiple_of(i * 256, 256), 256), :], NT, preferred_element_type=F32
+        )
+        for j in range(4):
+            qrows = pl.ds(pl.multiple_of(g * 256 + j * 64, 64), 64)
+            for t in range(2):
+                cols = pl.ds(pl.multiple_of(i * 256 + t * 128, 128), 128)
+                v = got[j * 64:(j + 1) * 64, lanes(t)]
+                lg_ref[qrows, cols] = v.astype(BF16)
+                is_ref[g, j:j + 1, cols] = jnp.sum(
+                    jnp.maximum(v, 0.0) * wcol_ref[qrows, :], axis=0, keepdims=True
+                )
 
     unit = lax.broadcasted_iota(jnp.int32, (256, 256), 0) == lax.broadcasted_iota(jnp.int32, (256, 256), 1)
     unit = jnp.where(unit, 1.0, 0.0).astype(BF16)
@@ -107,6 +96,8 @@
         got = lax.dot_general(unit, mqt[i], NT, preferred_element_type=F32).astype(BF16)
         for c in range(8):
             mq_ref[c, i] = got[c * 32:(c + 1) * 32, :]
+        index_part(0, i)
+        index_part(1, i)
         return carry
 
     lax.fori_loop(0, 8, turn, 0)
@@ -142,21 +133,21 @@
 
     def soft_piece(b, i, s_ref):
         r0 = pl.multiple_of(chip(b) * 256, 256)
-        rows = pl.ds(pl.multiple_of(i * 64, 64), 64)
-        reach = jnp.concatenate([posb_ref[...]] * 2, axis=0)
-        top = jnp.full((64, 128), FLOOR, F32)
+        rows = pl.ds(pl.multiple_of(i * 32, 32), 32)
+        reach = posb_ref[...]
+        top = jnp.full((32, 128), FLOOR, F32)
         for t in range(16):
             v = jnp.minimum(s_ref[rows, lanes(t)], reach + (0.5 - t * 128) * HUGE)
             s_ref[rows, lanes(t)] = v
             top = jnp.maximum(top, v)
-        mcol = jnp.broadcast_to(jnp.max(top, axis=1, keepdims=True), (64, 128))
-        total = jnp.zeros((64, 128), F32)
-        erows = pl.ds(pl.multiple_of(r0 + i * 64, 64), 64)
+        mcol = jnp.broadcast_to(jnp.max(top, axis=1, keepdims=True), (32, 128))
+        total = jnp.zeros((32, 128), F32)
+        erows = pl.ds(pl.multiple_of(r0 + i * 32, 32), 32)
         for t in range(16):
             e = jnp.exp2((s_ref[rows, lanes(t)] - mcol) * SCALE2)
             total = total + e
             e_ref[erows, lanes(t)] = e.astype(BF16)
-        lcol = jnp.broadcast_to(jnp.sum(total, axis=1, keepdims=True), (64, 128))
+        lcol = jnp.broadcast_to(jnp.sum(total, axis=1, keepdims=True), (32, 128))
         st_ref[rows, :] = jnp.where(lane == 0, mcol, lcol)
 
     def reach_of(b):
@@ -216,6 +207,9 @@
 
     def first(i, carry):
         score_quarter(0, i, s_a)
+        for j in range(2):
+            rows = pl.ds(pl.multiple_of(i * 256 + j * 128, 128), 128)
+            iqt_ref[:, rows] = jnp.transpose(iq[rows, :].astype(F32) * wcol_ref[rows, :]).astype(BF16)
         return carry
 
     lax.fori_loop(0, 4, first, 0)
@@ -225,8 +219,9 @@
         reach_of(b)
 
         for i in range(4):
-            soft_piece(b, i, s_now)
+            soft_piece(b, i * 2, s_now)
             score_quarter(jnp.minimum(b + 1, 7), i, s_next)
+            soft_piece(b, i * 2 + 1, s_now)
         send_stats(b)
 
         @pl.when(b >= LAG)
@@ -249,16 +244,17 @@
 
     target_block(5)
 
-    def index_rest(g, carry):
-        index_step(g, carry)
-
-        @pl.when(g == 2)
+    def index_rest(i, carry):
+        index_part(2, i)
+        index_part(3, i)
+
+        @pl.when(i == 4)
         def _():
             own_chip(0)
 
         return carry
 
-    lax.fori_loop(2, 4, index_rest, 0)
+    lax.fori_loop(0, 8, index_rest, 0)
     own_chip(1)
 
     row = lax.broadcasted_iota(jnp.int32, (16, 128), 0)
@@ -284,6 +280,13 @@
     for r in range(1, 16):
         to_keys(ist_mine, ist_all.at[r - 1], ist_ss, ist_rs, (k + r) % 16).start()
 
+    def turn_keys(i, carry):
+        for j in range(4):
+            rows = pl.ds(pl.multiple_of(i * 512 + j * 128, 128), 128)
+            ikt[:, rows] = jnp.transpose(ik[rows, :].astype(F32)).astype(BF16)
+        return carry
+
+    lax.fori_loop(0, 4, turn_keys, 0)
     target_block(6)
     target_block(7)
     own_chip(2)
@@ -326,7 +329,7 @@
                     )
             picked.append(pl.ds(pl.multiple_of(q0 * 64, 128), 128))
         gate = jnp.concatenate([sl_ref[rows, :] for rows in picked], axis=0)
-        both = jnp.dot(gate, ikc[...], preferred_element_type=F32)
+        both = jnp.transpose(lax.dot_general(ikt[...], gate, NT, preferred_element_type=F32))
         columns = jnp.zeros((64, 128), F32)
         for n, (off, rows) in enumerate(zip(offsets, picked)):
             got = both[n * 128:(n + 1) * 128, :]
@@ -384,13 +387,18 @@
     lax.fori_loop(0, 8, key_step, 0)
     z_join()
 
-    for i in range(4):
+    def key_chip(i):
         cross_y(i, kp_ref, kc_ref, kx_ref, ky_ref, kc_rs, kx_rs, ky_ss, ky_rs)
+
+    for i in range(3):
+        key_chip(i)
 
     for j in range(4):
         take(qg_recv.at[2 + j], qg_rs.at[4 + j])
     qg_part[0] = qg_part[0] + (qg_recv[2] + qg_recv[3]) + (qg_recv[4] + qg_recv[5])
     to_keys(qg_part.at[0], qg_xh, xh_ss, xh_rs, z * 2 + (1 - xh)).start()
+
+    key_chip(3)
 
     for j in range(3):
         take(ky_ref.at[j], ky_rs.at[j])
@@ -480,20 +488,16 @@
         pltpu.VMEM((2048, 128), BF16),
         pltpu.VMEM((16, 16, 2048), BF16),
         pltpu.VMEM((1024, 2048), BF16),
+        pltpu.VMEM((128, 2048), BF16),
     )
 
 
 def finish(qg_all, kg_all, qg_out, kg_out, wg_out):
-    for i in range(2):
+    for i in range(8):
         qg_out[i * 128:(i + 1) * 128, :] = qg_all[i, 0:128, :]
-    for i in range(4):
+        wg_out[i * 2:(i + 1) * 2, :] = qg_all[i, 128:130, 0:64]
+    for i in range(16):
         kg_out[i * 128:(i + 1) * 128, :] = kg_all[i]
-    for n in range(4):
-
-        @pl.when(pl.program_id(0) == n)
-        def _():
-            for i in range(2):
-                wg_out[n * 4 + i * 2:n * 4 + (i + 1) * 2, :] = qg_all[i, 128:130, 0:64]
 
 
 def shards(main_query, latent_keys, index_query, index_keys, index_weight, query_pos, kl_weight):
@@ -564,16 +568,8 @@
             jax.ShapeDtypeStruct((2048, 128), F32),
             jax.ShapeDtypeStruct((16, 64), F32),
         ),
-        grid=(4,),
-        in_specs=[
-            pl.BlockSpec((2, 136, 128), lambda n: (n, 0, 0)),
-            pl.BlockSpec((4, 128, 128), lambda n: (n, 0, 0)),
-        ],
-        out_specs=(
-            pl.BlockSpec((256, 128), lambda n: (n, 0)),
-            pl.BlockSpec((512, 128), lambda n: (n, 0)),
-            pl.BlockSpec((16, 64), lambda n: (0, 0)),
-        ),
+        in_specs=[vmem, vmem],
+        out_specs=(vmem, vmem, vmem),
         name="finish",
     )(query_blocks, key_blocks)
     return query_grad.reshape(16, 64, 128), key_grad, weight_grad

time: 76.2 us -> 72.3 us (0.949); the launches traced: 75.2 us -> 72.2 us
  Pallas kernels: 74.5 us -> 71.5 us
    pallas_call x1, Pallas kernels: 70.9 us -> 68.9 us  [shards(): pl.pallas_call(scoped, out_shape=(jax.ShapeDtypeStruct((8, 136, 128), F32...]
    pallas_call x1, Pallas kernels: 3.65 us -> 2.61 us  [shards(): pl.pallas_call(finish, out_shape=(jax.ShapeDtypeStruct((1024, 128), F32),...]
where the time goes in v5:
time: 72.3 us; the launch traced here: 72.2 us
  Pallas kernels  71.5 us (99%)
    pallas_call x1, Pallas kernels, shards(): pl.pallas_call(scoped, out_shape=(jax.ShapeDtypeStruct((8, 136, 128), F32...  68.9 us
    pallas_call x1, Pallas kernels, shards(): pl.pallas_call(finish, out_shape=(jax.ShapeDtypeStruct((1024, 128), F32),...  2.61 us

profile of v5, /device:TPU:1, one launch (start us, length us, event | category | flops | bytes accessed | tf_op | source)
XLA Modules:
  0.0 72.2 jit_solution(1344829302337297342)
XLA Ops:
  0.6 68.9 %fused_indexer_step.1 = (f32[8,136,128]{2,1,0:T(8,128)}, f32[16,128,128]{2,1,0:T(8,128)}) custom-call(s32[256]{0:T(256)} %refs_0_.1, f32[16]{0:T(128)} %refs_1_.1, bf16[8,576,256]{2,1,0:T(8,128)(2,1)} %bitcast.4, bf16[576,2048]{1,0:T(8,128)(2,1)} %bitcast.5, bf16[1024,128]{1,0:T(8,128)(2,1)} %bitcast.6, bf16[2048,128]{1,0:T(8,128)(2,1)} %refs_5_.1, ...), custom_call_target="tpu_custom_call" | custom-call | tf_op jit(solution)/shard_map/fused_indexer_step/pallas_call | solution.py:508
  69.6 2.6 %finish.1 = (f32[1024,128]{1,0:T(8,128)}, f32[2048,128]{1,0:T(8,128)}, f32[16,64]{1,0:T(8,128)}) custom-call(f32[8,136,128]{2,1,0:T(8,128)} %get-tuple-element.8.qg_all, f32[16,128,128]{2,1,0:T(8,128)} %get-tuple-element.9.kg_all), custom_call_target="tpu_custom_call" | custom-call | tf_op jit(solution)/shard_map/finish/pallas_call | solution.py:564

commit v6 on v5

--- a/solution.py
+++ b/solution.py
@@ -26,14 +26,14 @@
 
 def fused(
     pos_s, kl_s, mqt_hbm, lkt_hbm, iq, ik, iw,
-    qg_all, kg_all,
+    qg_hbm, kg_hbm,
     mqt, lkt_in, posb_ref,
     s_a, s_b, st_ref, stat_mine, stat_all,
     tp_ref, tc_ref, tx_ref, ty_ref,
     wpad_ref, wcol_ref, is_ref, ie_ref, ist_mine, ist_all,
     wgc_ref, qg_part, qg_recv, qg_four, qg_xh,
-    kp_ref, kc_ref, kx_ref, ky_ref,
-    mq_in, lk_in,
+    kp_ref, kc_ref, kx_ref, ky_ref, qg_all, kg_all,
+    mq_in, lk_in, qg_out, kg_out,
     stat_ss, stat_rs, ist_ss, ist_rs,
     tc_ss, tc_rs, tx_ss, tx_rs, ty_ss, ty_rs,
     qg_ss, qg_rs, xh_ss, xh_rs, qa_ss, qa_rs,
@@ -407,6 +407,13 @@
         shard = shard + ky_ref[j]
     kg_all[h] = jnp.transpose(shard)
 
+    def key_done(s):
+        pltpu.make_async_copy(kg_all.at[s], kg_hbm.at[s], kg_out.at[s]).start()
+
+    def query_done(off):
+        i = (z + off) % 8
+        pltpu.make_async_copy(qg_all.at[i], qg_hbm.at[i], qg_out.at[i]).start()
+
     def pass_on(s, peer, n):
         to_heads(kg_all.at[s], kg_all.at[s], ka_ss.at[n], ka_rs.at[s], peer).start()
 
@@ -445,15 +452,26 @@
         take(kg_all.at[s], ka_rs.at[s])
         pass_on(s, partner, 11 + off)
 
+    key_done(h)
+    for off in (1, 3, 2):
+        key_done(along_y(off))
+    for off in (0, 1, 3, 2):
+        key_done((1 - x) * 8 + ((y + off) % 4) * 2 + core)
     z_take(7, whole, 2)
     z_take(1, whole, 3)
-    z_take(4, front, 4)
-    z_take(5, whole, 5)
-    z_take(4, rear, 6)
-    z_take(3, whole, 7)
+    for off in (0, 1, 2, 6, 7):
+        query_done(off)
     for c in range(8):
         s = c * 2 + (1 - core)
         take(kg_all.at[s], ka_rs.at[s])
+        key_done(s)
+    z_take(4, front, 4)
+    z_take(4, rear, 6)
+    query_done(4)
+    z_take(5, whole, 5)
+    query_done(5)
+    z_take(3, whole, 7)
+    query_done(3)
 
     for b in range(8):
         take(stat_all.at[b], stat_ss.at[b])
@@ -475,6 +493,10 @@
     take(qg_xh, xh_ss)
     for n in range(15):
         take(kg_all.at[n], ka_ss.at[n])
+    for i in range(8):
+        pltpu.make_async_copy(qg_all.at[i], qg_hbm.at[i], qg_out.at[i]).wait()
+    for i in range(16):
+        pltpu.make_async_copy(kg_all.at[i], kg_hbm.at[i], kg_out.at[i]).wait()
 
 
 def scoped(*refs):
@@ -492,12 +514,25 @@
     )
 
 
-def finish(qg_all, kg_all, qg_out, kg_out, wg_out):
+def finish(qg_hbm, kg_hbm, qg_out, kg_out, wg_out, qg, kg, q_in, k_in, q_to, k_to):
+    qs = [pltpu.make_async_copy(qg_hbm.at[pl.ds(i * 4, 4)], qg.at[pl.ds(i * 4, 4)], q_in.at[i]) for i in range(2)]
+    ks = [pltpu.make_async_copy(kg_hbm.at[pl.ds(i * 4, 4)], kg.at[pl.ds(i * 4, 4)], k_in.at[i]) for i in range(4)]
+    for copy in qs + ks:
+        copy.start()
+    outs = []
+    for i in range(2):
+        qs[i].wait()
+        for j in range(i * 4, i * 4 + 4):
+            outs.append(pltpu.make_async_copy(qg.at[j, pl.ds(0, 128)], qg_out.at[j], q_to.at[j]))
+            outs[-1].start()
+    for i in range(4):
+        ks[i].wait()
+        outs.append(pltpu.make_async_copy(kg.at[pl.ds(i * 4, 4)], kg_out.at[pl.ds(i * 4, 4)], k_to.at[i]))
+        outs[-1].start()
     for i in range(8):
-        qg_out[i * 128:(i + 1) * 128, :] = qg_all[i, 0:128, :]
-        wg_out[i * 2:(i + 1) * 2, :] = qg_all[i, 128:130, 0:64]
-    for i in range(16):
-        kg_out[i * 128:(i + 1) * 128, :] = kg_all[i]
+        wg_out[i * 2:(i + 1) * 2, :] = qg[i, 128:130, 0:64]
+    for copy in outs:
+        copy.wait()
 
 
 def shards(main_query, latent_keys, index_query, index_keys, index_weight, query_pos, kl_weight):
@@ -512,7 +547,7 @@
             jax.ShapeDtypeStruct((16, 128, 128), F32),
         ),
         in_specs=[smem, smem, hbm, hbm, vmem, vmem, vmem],
-        out_specs=(vmem, vmem),
+        out_specs=(hbm, hbm),
         scratch_shapes=[
             pltpu.VMEM((8, 576, 256), BF16),
             pltpu.VMEM((576, 2048), BF16),
@@ -541,7 +576,9 @@
             pltpu.VMEM((8, 128, 128), F32),
             pltpu.VMEM((4, 128, 128), F32),
             pltpu.VMEM((3, 128, 128), F32),
-            dma((8,)), dma,
+            pltpu.VMEM((8, 136, 128), F32),
+            pltpu.VMEM((16, 128, 128), F32),
+            dma((8,)), dma, dma((8,)), dma((16,)),
             dma((8,)), dma((8,)), dma, dma,
             dma((8,)), dma((8,)), dma((4,)), dma((4,)), dma((3,)), dma((3,)),
             dma((8,)), dma((8,)), dma, dma, dma((8,)), dma((8,)),
@@ -564,15 +601,20 @@
     query_grad, key_grad, weight_grad = pl.pallas_call(
         finish,
         out_shape=(
-            jax.ShapeDtypeStruct((1024, 128), F32),
-            jax.ShapeDtypeStruct((2048, 128), F32),
+            jax.ShapeDtypeStruct((8, 128, 128), F32),
+            jax.ShapeDtypeStruct((16, 128, 128), F32),
             jax.ShapeDtypeStruct((16, 64), F32),
         ),
-        in_specs=[vmem, vmem],
-        out_specs=(vmem, vmem, vmem),
+        in_specs=[hbm, hbm],
+        out_specs=(hbm, hbm, vmem),
+        scratch_shapes=[
+            pltpu.VMEM((8, 136, 128), F32),
+            pltpu.VMEM((16, 128, 128), F32),
+            dma((2,)), dma((4,)), dma((8,)), dma((4,)),
+        ],
         name="finish",
     )(query_blocks, key_blocks)
-    return query_grad.reshape(16, 64, 128), key_grad, weight_grad
+    return query_grad.reshape(16, 64, 128), key_grad.reshape(2048, 128), weight_grad
 
 
 def solution(mesh):

time: 72.3 us -> 72.4 us (level)
  no operation moved by 1% of the time
where the time goes in v6:
time: 72.4 us; the launch traced here: 72.3 us
  Pallas kernels  71.7 us (99%)
    pallas_call x1, Pallas kernels, shards(): pl.pallas_call(scoped, out_shape=(jax.ShapeDtypeStruct((8, 136, 128), F32...  68.6 us
    pallas_call x1, Pallas kernels, shards(): pl.pallas_call(finish, out_shape=(jax.ShapeDtypeStruct((8, 128, 128), F32...  3.08 us

profile of v6, /device:TPU:1, one launch (start us, length us, event | category | flops | bytes accessed | tf_op | source)
XLA Modules:
  0.0 72.3 jit_solution(3307091132056146663)
XLA Ops:
  0.6 68.6 %fused_indexer_step.1 = (f32[8,136,128]{2,1,0:T(8,128)}, f32[16,128,128]{2,1,0:T(8,128)}) custom-call(s32[256]{0:T(256)} %refs_0_.1, f32[16]{0:T(128)} %refs_1_.1, bf16[8,576,256]{2,1,0:T(8,128)(2,1)} %bitcast.5, bf16[576,2048]{1,0:T(8,128)(2,1)} %bitcast.6, bf16[1024,128]{1,0:T(8,128)(2,1)} %bitcast.7, bf16[2048,128]{1,0:T(8,128)(2,1)} %refs_5_.1, ...), custom_call_target="tpu_custom_call" | custom-call | tf_op jit(solution)/shard_map/fused_indexer_step/pallas_call | solution.py:543
  69.2 3.1 %finish.1 = (f32[8,128,128]{2,1,0:T(8,128)}, f32[16,128,128]{2,1,0:T(8,128)}, f32[16,64]{1,0:T(8,128)}) custom-call(f32[8,136,128]{2,1,0:T(8,128)} %get-tuple-element.8.qg_hbm, f32[16,128,128]{2,1,0:T(8,128)} %get-tuple-element.9.kg_hbm), custom_call_target="tpu_custom_call" | custom-call | tf_op jit(solution)/shard_map/finish/pallas_call | solution.py:601

commit v7 on v5

--- a/solution.py
+++ b/solution.py
@@ -549,7 +549,7 @@
             dma((15,)), dma((16,)),
         ],
         compiler_params=pltpu.CompilerParams(
-            collective_id=0, has_side_effects=True, vmem_limit_bytes=60 * 1024 * 1024
+            collective_id=0, has_side_effects=True, vmem_limit_bytes=50 * 1024 * 1024
         ),
         name="fused_indexer_step",
     )(
@@ -570,6 +570,7 @@
         ),
         in_specs=[vmem, vmem],
         out_specs=(vmem, vmem, vmem),
+        compiler_params=pltpu.CompilerParams(vmem_limit_bytes=8 * 1024 * 1024),
         name="finish",
     )(query_blocks, key_blocks)
     return query_grad.reshape(16, 64, 128), key_grad, weight_grad

time: 72.3 us -> 73.2 us (1.012)
  local copies, waits for them, and re-layouts: 0 us -> 4.01 us
  Pallas kernels: 71.5 us -> 68.3 us
    unnamed x0 -> x10, local copies, waits for them, and re-layouts: none -> 4.01 us
    pallas_call x1, Pallas kernels: 68.9 us -> 67 us  [shards(): pl.pallas_call(scoped, out_shape=(jax.ShapeDtypeStruct((8, 136, 128), F32...]
    pallas_call x1, Pallas kernels: 2.61 us -> 1.24 us  [shards(): pl.pallas_call(finish, out_shape=(jax.ShapeDtypeStruct((1024, 128), F32),...]
where the time goes in v7:
time: 73.2 us; the launch traced here: 72.9 us
  Pallas kernels  68.3 us (93%)
  local copies, waits for them, and re-layouts  4.01 us (5%)
    pallas_call x1, Pallas kernels, shards(): pl.pallas_call(scoped, out_shape=(jax.ShapeDtypeStruct((8, 136, 128), F32...  67 us
    unnamed x10, local copies, waits for them, and re-layouts  4.01 us

profile of v7, /device:TPU:1, one launch (start us, length us, event | category | flops | bytes accessed | tf_op | source)
XLA Modules:
  0.0 72.9 jit_solution(15177360846882866396)
XLA Ops:
  0.6 0.0 copy-start
  0.6 1.0 %copy-done = bf16[2048,128]{1,0:T(8,128)(2,1)S(1)} copy-done((bf16[2048,128]{1,0:T(8,128)(2,1)S(1)}, bf16[2048,128]{1,0:T(8,128)(2,1)}, u32[]{:S(2)}) %copy-start) | copy-done | bytes 524312
  1.7 0.0 copy-start.1
  1.7 0.9 %copy-done.1 = bf16[16,64,128]{2,1,0:T(8,128)(2,1)S(1)} copy-done((bf16[16,64,128]{2,1,0:T(8,128)(2,1)S(1)}, bf16[16,64,128]{2,1,0:T(8,128)(2,1)}, u32[]{:S(2)}) %copy-start.1) | copy-done | bytes 262168
  2.6 0.0 copy-start.2
  2.6 0.7 copy-done.2
  3.3 0.0 copy-start.3
  3.3 0.7 copy-done.3
  4.0 0.0 copy-start.4
  4.0 0.7 copy-done.4
  4.7 67.0 %fused_indexer_step.1 = (f32[8,136,128]{2,1,0:T(8,128)S(1)}, f32[16,128,128]{2,1,0:T(8,128)S(1)}) custom-call(s32[256]{0:T(256)S(1)} %copy-done.3, f32[16]{0:T(128)S(1)} %copy-done.4, bf16[8,576,256]{2,1,0:T(8,128)(2,1)} %bitcast.5, bf16[576,2048]{1,0:T(8,128)(2,1)} %bitcast.6, bf16[1024,128]{1,0:T(8,128)(2,1)S(1)} %bitcast.4, ...), custom_call_target="tpu_custom_call" | custom-call | tf_op jit(solution)/shard_map/fused_indexer_step/pallas_call | solution.py:508
  71.7 1.2 %finish.1 = (f32[1024,128]{1,0:T(8,128)}, f32[2048,128]{1,0:T(8,128)}, f32[16,64]{1,0:T(8,128)}) custom-call(f32[8,136,128]{2,1,0:T(8,128)S(1)} %get-tuple-element.8.qg_all, f32[16,128,128]{2,1,0:T(8,128)S(1)} %get-tuple-element.9.kg_all), custom_call_target="tpu_custom_call" | custom-call | tf_op jit(solution)/shard_map/finish/pallas_call | solution.py:564
Async XLA Ops:
  0.6 1.0 %copy-start = (bf16[2048,128]{1,0:T(8,128)(2,1)S(1)}, bf16[2048,128]{1,0:T(8,128)(2,1)}, u32[]{:S(2)}) copy-start(bf16[2048,128]{1,0:T(8,128)(2,1)} %refs_5_.1) | copy-start | bytes 1572868
  1.7 0.9 %copy-start.1 = (bf16[16,64,128]{2,1,0:T(8,128)(2,1)S(1)}, bf16[16,64,128]{2,1,0:T(8,128)(2,1)}, u32[]{:S(2)}) copy-start(bf16[16,64,128]{2,1,0:T(8,128)(2,1)} %param.9) | copy-start | bytes 786436
  2.6 0.7 copy-start.2
  3.3 0.7 copy-start.3
  4.0 0.7 copy-start.4
